TPU v7x, 32 devices: a whole 2x2x4 slice. The times are simulated.
32 devices in a mesh: dp: 16 (over z, x, core), tensor: 2 (over y).
Axes of the slice: x: 2, y: 2, z: 4, core: 2. Of those that a mesh axis runs over, the one named last changes fastest.
Arguments:
- tokens: bfloat16 [320, 6144], P('dp', 'tensor'), may hold values from -6 to 6
- route_ids: int32 [320, 2], replicated, may hold values from 0 to 3, all different within a row
- route_probs: bfloat16 [320, 2], replicated, may hold values from 0.099609375 to 1
- w_gate: bfloat16 [4, 6144, 8192], P(None, 'tensor', 'dp'), may hold values from -0.078125 to 0.078125
- w_up: bfloat16 [4, 6144, 8192], P(None, 'tensor', 'dp'), may hold values from -0.078125 to 0.078125
- w_down: bfloat16 [4, 8192, 6144], P(None, 'dp', 'tensor'), may hold values from -0.0625 to 0.0625
Outputs:
- mixed_out: bfloat16 [320, 6144], P('dp', 'tensor')
Inputs may be any that keep to these rules, and one draw needn't show every extreme that they name: `route_ids`: each row names 2 different experts, and every expert is named by some row.
All inputs are finite; a program needn't handle non-finite values.
Results may differ from a plain program's by a relative error of at most 0.0049.
Values may be sent and summed in bfloat16 or wider, within the bound.
No kernel may reach another device: no remote copies, remote signals or barrier semaphores. Data moves between devices by JAX's collectives and lax.ppermute only.
A program may use at most 128 MiB of HBM per device.

v0:
```python
import functools

import jax
import jax.numpy as jnp
from jax import lax
from jax.experimental import pallas as pl
from jax.experimental.pallas import tpu as pltpu
from jax.sharding import PartitionSpec as P


BF = jnp.bfloat16
F32 = jnp.float32
LIMIT = 10 * 1024 * 1024


def tile_of(width, most):
    tile = min(width, most)
    while width % tile:
        tile //= 2
    return tile


def copies_of(source, target, sem):
    count, depth = target.shape[0], target.shape[1] // 2
    copies = []
    for e in range(count):
        for part in range(2):
            piece = pl.ds(part * depth, depth)
            copies.append(pltpu.make_async_copy(source(e).at[piece], target.at[e, piece], sem.at[e, part]))
    return copies


def fetch_kernel(part, source_ref, target_ref, sem_ref):
    copies = copies_of(lambda e: source_ref.at[e, part], target_ref, sem_ref)
    for copy in copies:
        copy.start()
    for copy in copies:
        copy.wait()


def in_hbm(w):
    return pltpu.with_memory_space_constraint(w, pltpu.HBM)


def fetch(w, part):
    shape = w.shape[:1] + w.shape[2:]
    return pl.pallas_call(
        functools.partial(fetch_kernel, part),
        in_specs=[pl.BlockSpec(memory_space=pltpu.HBM)],
        out_specs=pl.BlockSpec(memory_space=pltpu.VMEM),
        out_shape=pltpu.VMEM(shape, w.dtype),
        scratch_shapes=[pltpu.SemaphoreType.DMA((w.shape[0], 2))],
        cost_estimate=pl.CostEstimate(flops=0, bytes_accessed=4 * w.size // w.shape[1], transcendentals=0),
        compiler_params=pltpu.CompilerParams(vmem_limit_bytes=LIMIT),
        name="fetch",
    )(in_hbm(w))


def order_kernel(lines, chip_rows, where_ref, ids_ref, probs_ref, wu_ref, ids_out, probs_out, fetched_ref, sem_ref):
    copies = copies_of(lambda e: wu_ref.at[e], fetched_ref, sem_ref)
    for copy in copies:
        copy.start()
    top, token_count = ids_ref.shape
    row = lax.broadcasted_iota(jnp.int32, (chip_rows, token_count), 0)
    column = lax.broadcasted_iota(jnp.int32, (chip_rows, token_count), 1)
    for i, (xr, k) in enumerate((xr, k) for xr in range(2) for k in range(lines)):
        source = jnp.bitwise_xor(where_ref[2], 2 * k + xr) * chip_rows
        mine = column == row + source
        rows = slice(i * chip_rows, (i + 1) * chip_rows)
        for k in range(top):
            ids = jnp.where(mine, ids_ref[k : k + 1, :].astype(F32), 0.0)
            probs = jnp.where(mine, probs_ref[k : k + 1, :].astype(F32), 0.0)
            ids_out[rows, k : k + 1] = jnp.sum(ids, axis=1, keepdims=True).astype(jnp.int32)
            probs_out[rows, k : k + 1] = jnp.sum(probs, axis=1, keepdims=True)
    for copy in copies:
        copy.wait()


def order(lines, chip_rows, where, ids, probs, w_up):
    count = w_up.shape[0] - w_up.shape[0] // 2
    token_count, top = ids.shape
    inside = pl.BlockSpec(memory_space=pltpu.VMEM)
    return pl.pallas_call(
        functools.partial(order_kernel, lines, chip_rows),
        in_specs=[pl.BlockSpec(memory_space=pltpu.SMEM), inside, inside, pl.BlockSpec(memory_space=pltpu.HBM)],
        out_specs=[inside] * 3,
        out_shape=[
            jax.ShapeDtypeStruct((token_count, top), jnp.int32),
            jax.ShapeDtypeStruct((token_count, top), F32),
            pltpu.VMEM((count,) + w_up.shape[1:], w_up.dtype),
        ],
        scratch_shapes=[pltpu.SemaphoreType.DMA((count, 2))],
        cost_estimate=pl.CostEstimate(flops=0, bytes_accessed=4 * w_up.size // 2, transcendentals=0),
        compiler_params=pltpu.CompilerParams(vmem_limit_bytes=LIMIT),
        name="order",
    )(where, ids.T, probs.T, in_hbm(w_up))


def share_out(n, me, acc_ref, keep_ref, send_ref):
    rows = keep_ref.shape[1]
    for s in range(n):
        begin = pl.multiple_of(lax.rem(me + s, n) * rows, rows)
        block = acc_ref[:, pl.ds(begin, rows), :]
        if s == 0:
            keep_ref[...] = block
        else:
            send_ref[s - 1] = block.astype(BF)


def gate_kernel(n, stage, where_ref, ids_ref, rows_ref, wg_ref, *refs):
    copies = []
    if stage == 0:
        wu_ref, acc_ref, fetched_ref, sem_ref = refs
        last = wu_ref.shape[0] - fetched_ref.shape[0]
        copies = copies_of(lambda e: wu_ref.at[last + e], fetched_ref, sem_ref)
    else:
        base_ref, keep_ref, send_ref, acc_ref = refs
    for copy in copies:
        copy.start()
    half = where_ref[0] if stage == 0 else 1 - where_ref[0]
    tile = tile_of(wg_ref.shape[3], 256)
    for e in range(wg_ref.shape[0]):
        for j in range(wg_ref.shape[3] // tile):
            columns = pl.ds(j * tile, tile)
            block = jnp.dot(rows_ref[...], wg_ref[e, half, :, columns], preferred_element_type=F32)
            for k in range(acc_ref.shape[0]):
                value = block if stage == 0 else block + base_ref[k, :, columns]
                if e > 0:
                    value = jnp.where(ids_ref[:, k : k + 1] == e, value, acc_ref[k, :, columns])
                acc_ref[k, :, columns] = value
    if stage == 1:
        share_out(n, where_ref[1], acc_ref, keep_ref, send_ref)
    for copy in copies:
        copy.wait()


def gate_gemm(n, stage, where, ids, rows, w_gate, extra):
    token_count, top = ids.shape
    experts, _, half, hidden = w_gate.shape
    inside = pl.BlockSpec(memory_space=pltpu.VMEM)
    outside = pl.BlockSpec(memory_space=pltpu.HBM)
    whole = (top, token_count, hidden)
    count = experts // 2
    if stage == 0:
        extra, extra_spec = in_hbm(extra), outside
        out_shape = [jax.ShapeDtypeStruct(whole, F32), pltpu.VMEM((count, 2, half, hidden), BF)]
        scratch = [pltpu.SemaphoreType.DMA((count, 2))]
    else:
        extra_spec = inside
        out_shape = [
            jax.ShapeDtypeStruct((top, token_count // n, hidden), F32),
            jax.ShapeDtypeStruct((n - 1, top, token_count // n, hidden), BF),
        ]
        scratch = [pltpu.VMEM(whole, F32)]
    return pl.pallas_call(
        functools.partial(gate_kernel, n, stage),
        in_specs=[pl.BlockSpec(memory_space=pltpu.SMEM)] + [inside] * 3 + [extra_spec],
        out_specs=[inside] * len(out_shape),
        scratch_shapes=scratch,
        out_shape=out_shape,
        cost_estimate=pl.CostEstimate(
            flops=2 * token_count * half * hidden * experts,
            bytes_accessed=2 * experts * half * hidden,
            transcendentals=0,
        ),
        compiler_params=pltpu.CompilerParams(vmem_limit_bytes=LIMIT),
        name="gate_gemm",
    )(where, ids, rows, w_gate, extra)


def up_kernel(n, part, where_ref, ids_ref, own_ref, other_ref, *refs):
    weight_refs, (keep_ref, send_ref, acc_ref) = refs[:-3], refs[-3:]
    half = where_ref[0]
    tile = acc_ref.shape[2]
    columns = pl.ds(part * tile, tile)
    e = 0
    for w_ref in weight_refs:
        for i in range(w_ref.shape[0]):
            block = jnp.dot(own_ref[...], w_ref[i, half, :, columns], preferred_element_type=F32)
            block += jnp.dot(other_ref[...], w_ref[i, 1 - half, :, columns], preferred_element_type=F32)
            for k in range(acc_ref.shape[0]):
                value = block
                if e > 0:
                    value = jnp.where(ids_ref[:, k : k + 1] == e, value, acc_ref[k])
                acc_ref[k] = value
            e += 1
    share_out(n, where_ref[1], acc_ref, keep_ref, send_ref)


def up_gemm(n, part, parts, where, ids, own, other, weights):
    token_count, top = ids.shape
    half, hidden = weights[0].shape[2:]
    experts = sum(w.shape[0] for w in weights)
    rows = token_count // n
    tile = hidden // parts
    inside = pl.BlockSpec(memory_space=pltpu.VMEM)
    return pl.pallas_call(
        functools.partial(up_kernel, n, part),
        in_specs=[pl.BlockSpec(memory_space=pltpu.SMEM)] + [inside] * (3 + len(weights)),
        out_specs=[inside] * 2,
        scratch_shapes=[pltpu.VMEM((top, token_count, tile), F32)],
        out_shape=[
            jax.ShapeDtypeStruct((top, rows, tile), F32),
            jax.ShapeDtypeStruct((n - 1, top, rows, tile), BF),
        ],
        cost_estimate=pl.CostEstimate(
            flops=4 * token_count * half * tile * experts,
            bytes_accessed=4 * experts * half * tile,
            transcendentals=0,
        ),
        compiler_params=pltpu.CompilerParams(vmem_limit_bytes=LIMIT),
        name="up_gemm",
    )(where, ids, own, other, *weights)


def pick_rows(n, me, ids_ref, hidden_refs, rows_ref):
    top, rows, depth = hidden_refs[0].shape
    for s in range(n):
        begin = pl.multiple_of(lax.rem(me + n - s, n) * rows, rows)
        for e in range(rows_ref.shape[0]):
            total = jnp.zeros((rows, depth), F32)
            for k in range(top):
                chosen = ids_ref[pl.ds(begin, rows), k : k + 1] == e
                total = jnp.where(chosen, hidden_refs[s][k].astype(F32), total)
            rows_ref[e, pl.ds(begin, rows), :] = total.astype(BF)


def share_of(ids_ref, probs_ref, e):
    share = jnp.zeros((ids_ref.shape[0], 1), F32)
    for k in range(ids_ref.shape[1]):
        share = jnp.where(ids_ref[:, k : k + 1] == e, probs_ref[:, k : k + 1], share)
    return share


def pick_kernel(n, where_ref, ids_ref, *refs):
    pick_rows(n, where_ref[1], ids_ref, refs[:-1], refs[-1])


def pick(n, where, ids, hiddens, experts):
    inside = pl.BlockSpec(memory_space=pltpu.VMEM)
    return pl.pallas_call(
        functools.partial(pick_kernel, n),
        in_specs=[pl.BlockSpec(memory_space=pltpu.SMEM)] + [inside] * (1 + n),
        out_specs=inside,
        out_shape=jax.ShapeDtypeStruct((experts, ids.shape[0], hiddens[0].shape[2]), BF),
        compiler_params=pltpu.CompilerParams(vmem_limit_bytes=LIMIT),
        name="pick",
    )(where, ids, *hiddens)


def first_kernel(n, where_ref, ids_ref, probs_ref, *refs):
    hidden_refs, (wd_ref, out_ref, rows_ref) = refs[:n], refs[n:]
    pick_rows(n, where_ref[1], ids_ref, hidden_refs, rows_ref)
    half = out_ref.shape[2]
    tile = tile_of(half, 512)
    for e in range(wd_ref.shape[0]):
        share = share_of(ids_ref, probs_ref, e)
        for own in range(2):
            side = where_ref[0] if own else 1 - where_ref[0]
            for j in range(half // tile):
                columns = pl.ds(j * tile, tile)
                source = pl.ds(pl.multiple_of(side * half + j * tile, 128), tile)
                term = share * jnp.dot(rows_ref[e], wd_ref[e, :, source], preferred_element_type=F32)
                if e > 0:
                    term += out_ref[own, :, columns]
                out_ref[own, :, columns] = term


def first_down(n, where, ids, probs, hiddens, w_down):
    token_count = ids.shape[0]
    experts, _, width = w_down.shape
    depth = hiddens[0].shape[2]
    inside = pl.BlockSpec(memory_space=pltpu.VMEM)
    return pl.pallas_call(
        functools.partial(first_kernel, n),
        in_specs=[pl.BlockSpec(memory_space=pltpu.SMEM)] + [inside] * (3 + n),
        out_specs=inside,
        scratch_shapes=[pltpu.VMEM((experts, token_count, depth), BF)],
        out_shape=jax.ShapeDtypeStruct((2, token_count, width // 2), F32),
        cost_estimate=pl.CostEstimate(
            flops=2 * token_count * width * depth * experts,
            bytes_accessed=2 * experts * width * depth,
            transcendentals=0,
        ),
        compiler_params=pltpu.CompilerParams(vmem_limit_bytes=LIMIT),
        name="first_down",
    )(where, ids, probs, *hiddens, w_down)


def last_kernel(own, begin, where_ref, ids_ref, probs_ref, rows_ref, wd_ref, *refs):
    base_ref, (out_ref, acc_ref) = (refs[0] if len(refs) > 2 else None), refs[-2:]
    side = where_ref[0] if own else 1 - where_ref[0]
    experts, _, width = wd_ref.shape
    half = width // 2
    tile = tile_of(out_ref.shape[1], 256)
    for e in range(experts):
        share = share_of(ids_ref, probs_ref, e)
        for j in range(out_ref.shape[1] // tile):
            columns = pl.ds(j * tile, tile)
            source = pl.ds(pl.multiple_of(side * half + begin + j * tile, 128), tile)
            term = share * jnp.dot(rows_ref[e], wd_ref[e, :, source], preferred_element_type=F32)
            if e > 0:
                term += acc_ref[:, columns]
            elif base_ref is not None:
                term += base_ref[int(own), :, begin + j * tile : begin + (j + 1) * tile]
            if e < experts - 1:
                acc_ref[:, columns] = term
            else:
                out_ref[:, columns] = term


def last_down(where, ids, probs, rows, w_down, base, own, begin, end):
    token_count = ids.shape[0]
    experts, depth = w_down.shape[0], rows.shape[2]
    inside = pl.BlockSpec(memory_space=pltpu.VMEM)
    return pl.pallas_call(
        functools.partial(last_kernel, own, begin),
        in_specs=[pl.BlockSpec(memory_space=pltpu.SMEM)] + [inside] * (4 + len(base)),
        out_specs=inside,
        scratch_shapes=[pltpu.VMEM((token_count, end - begin), F32)],
        out_shape=jax.ShapeDtypeStruct((token_count, end - begin), F32),
        cost_estimate=pl.CostEstimate(
            flops=2 * token_count * (end - begin) * depth * experts,
            bytes_accessed=2 * experts * (end - begin) * depth,
            transcendentals=0,
        ),
        compiler_params=pltpu.CompilerParams(vmem_limit_bytes=LIMIT),
        name="down_own" if own else "down_other",
    )(where, ids, probs, rows, w_down, *base)


def sum_kernel(kept_ref, arrived_ref, out_ref):
    out_ref[...] = kept_ref[...] + arrived_ref[...].astype(F32)


def own_sum(kept, arrived):
    inside = pl.BlockSpec(memory_space=pltpu.VMEM)
    return pl.pallas_call(
        sum_kernel,
        in_specs=[inside] * 2,
        out_specs=inside,
        out_shape=jax.ShapeDtypeStruct(kept.shape, F32),
        compiler_params=pltpu.CompilerParams(vmem_limit_bytes=LIMIT),
        name="own_sum",
    )(kept, arrived)


def layer(tokens, route_ids, route_probs, w_gate, w_up, w_down):
    members = lax.axis_size("dp")
    n = lax.axis_size("tensor")
    lines = members // 4
    place = lax.axis_index("dp")
    side = place % 2
    me = lax.axis_index("tensor")
    where = jnp.stack([side, me, place // 2]).astype(jnp.int32)
    local_rows, width = tokens.shape
    half = width // 2
    first = side == 0
    experts, _, hidden_width = w_gate.shape
    w_gate = w_gate.reshape(experts, 2, half, hidden_width)
    w_up = w_up.reshape(experts, 2, half, hidden_width)
    chip_rows = 2 * local_rows
    parts = 2 if hidden_width % 256 == 0 else 1
    depth = hidden_width // parts
    cut = half // 128 * 2 // 3 * 128
    middle = (half // 128 + 1) // 2 * 128

    def flip(x, bits):
        return lax.ppermute(x, "dp", [(i, i ^ bits) for i in range(members)])

    def on_chip(x):
        return flip(x, 1)

    def over_x(x):
        return flip(x, 2)

    def over_z(x, k):
        return flip(x, 4 * k)

    def over_tensor(x):
        return [lax.ppermute(x[s - 1], "tensor", [(i, (i + s) % n) for i in range(n)]) for s in range(1, n)]

    def pair(mine, theirs, axis):
        return jnp.concatenate(
            [jnp.where(first, mine, theirs), jnp.where(first, theirs, mine)], axis=axis
        )

    def added(keep, arrived):
        for part in arrived:
            keep = keep + part.astype(F32)
        return keep

    left, right = tokens[:, :half], tokens[:, half:]
    theirs = on_chip(jnp.where(first, right, left))
    block = pair(jnp.where(first, left, right), theirs, 0)
    near, far = block[:, :cut], block[:, cut:]
    near_line = [near] + [over_z(near, k) for k in range(1, lines)]
    far_other = over_x(far)
    far_pair = [far, far_other]
    near_all = jnp.concatenate(near_line, axis=0)
    far_both = jnp.concatenate(far_pair, axis=0)
    near, w_up, where = lax.optimization_barrier((near, w_up, where))
    ids, probs, up_low = order(lines, chip_rows, where, route_ids, route_probs, w_up)
    near_all, far_both, w_gate, up_low = lax.optimization_barrier((near_all, far_both, w_gate, up_low))
    w_gate = fetch(w_gate.reshape(experts, 1, 2 * half, hidden_width), 0).reshape(experts, 2, half, hidden_width)
    near_other = over_x(near_all)
    far_line = [far_both] + [over_z(far_both, k) for k in range(1, lines)]
    near_other, far_line, w_gate = lax.optimization_barrier((near_other, far_line, w_gate))
    far_all = [jnp.concatenate([f[xr * chip_rows : (xr + 1) * chip_rows] for f in far_line], axis=0) for xr in range(2)]
    own = jnp.concatenate(
        [jnp.concatenate([near_all, near_other], axis=0), jnp.concatenate(far_all, axis=0)], axis=1
    )
    other = on_chip(own)

    base, up_high = gate_gemm(n, 0, where, ids, own, w_gate, w_up)
    keep_gate, send_gate = gate_gemm(n, 1, where, ids, other, w_gate, base)
    gate_arrived = over_tensor(send_gate)
    ups, up_arrived = [], []
    for part in range(parts):
        keep, send = up_gemm(n, part, parts, where, ids, own, other, [up_low, up_high])
        if part == parts - 1:
            send, w_down = lax.optimization_barrier((send, w_down))
            w_down = w_down.reshape(experts, parts, depth, width)
        ups.append(keep)
        up_arrived.append(over_tensor(send))
    down_parts, hiddens = [], []
    for part in range(parts):
        columns = slice(part * depth, (part + 1) * depth)
        if part > 0:
            w_down, hiddens[part - 1][0] = lax.optimization_barrier((w_down, hiddens[part - 1][0]))
        down_parts.append(fetch(w_down, part))
        up_arrived[part], down_parts[part] = lax.optimization_barrier((up_arrived[part], down_parts[part]))
        gate_sum = added(keep_gate[:, :, columns], [g[:, :, columns] for g in gate_arrived])
        up_sum = added(ups[part], up_arrived[part])
        hidden = (gate_sum * jax.nn.sigmoid(gate_sum) * up_sum).astype(BF)
        hiddens.append([hidden] + over_tensor([hidden] * (n - 1)))

    downs = []
    if parts > 1:
        downs = [first_down(n, where, ids, probs, hiddens[0], down_parts[0])]
    rows = pick(n, where, ids, hiddens[-1], experts)
    spans = ((0, middle), (middle, half))
    away = []
    for begin, end in spans:
        part = last_down(where, ids, probs, rows, down_parts[-1], downs, False, begin, end)
        part, rows = lax.optimization_barrier((part, rows))
        away.append(on_chip(part))
    kept, sent = [], []
    for i, (begin, end) in enumerate(spans):
        stay = last_down(where, ids, probs, rows, down_parts[-1], downs, True, begin, end)
        total = (stay + away[i]).reshape(2, lines, chip_rows, end - begin)
        part, rows = lax.optimization_barrier((total[1].astype(BF), rows))
        kept.append(total[0])
        sent.append(over_x(part))
    outs = []
    for i in range(len(spans)):
        line = kept[i] + sent[i].astype(F32)
        arrived = [over_z(line[k].astype(BF), k) for k in range(1, lines)]
        mine = own_sum(kept[i][0], sent[i][0])
        outs.append(added(mine, arrived))
    mixed = jnp.concatenate(outs, axis=1).astype(BF)
    upper, lower = mixed[:local_rows], mixed[local_rows:]
    others = on_chip(jnp.where(first, lower, upper))
    return pair(jnp.where(first, upper, lower), others, 1)


def solution(mesh):
    placed = (
        P("dp", "tensor"),
        P(),
        P(),
        P(None, "tensor", "dp"),
        P(None, "tensor", "dp"),
        P(None, "dp", "tensor"),
    )
    return jax.shard_map(layer, mesh=mesh, in_specs=placed, out_specs=P("dp", "tensor"), check_vma=False)
```

profile of v0, /device:TPU:0, one launch (start us, length us, event | category | flops | bytes accessed | tf_op | source)
XLA Modules:
  0.0 95.8 jit_solution(1108767081100366170)
XLA Ops:
  0.0 0.9 broadcast_select_fusion.6
  0.9 0.6 collective-permute-start
  1.6 0.8 collective-permute-done
  2.4 0.9 broadcast_select_fusion.4
  3.4 2.9 %collective-permute-start.4 = (bf16[40,512]{1,0:T(8,128)(2,1)S(1)}, bf16[40,512]{1,0:T(8,128)(2,1)S(1)}, u32[]{:S(2)}, u32[]{:S(2)}) collective-permute-start(bf16[40,512]{1,0:T(8,128)(2,1)S(1)} %pad_maximum_fusion.5), channel_id=1, source_target_pairs={{0,4},{2,6},{4,0},{6,2},{8,12},{10,14},{12,8},{14,10},{16,20},{18,... | collective-permute-start | bytes 122888 | tf_op jit(solution)/shard_map/ppermute | solution.py:369
  6.3 3.7 %collective-permute-start.3 = (bf16[40,1024]{1,0:T(8,128)(2,1)S(1)}, bf16[40,1024]{1,0:T(8,128)(2,1)S(1)}, u32[]{:S(2)}, u32[]{:S(2)}) collective-permute-start(bf16[40,1024]{1,0:T(8,128)(2,1)S(1)} %fusion), channel_id=1, source_target_pairs={{0,24},{2,26},{4,28},{6,30},{8,16},{10,18},{12,20},{14,22},{16,8},... | collective-permute-start | bytes 245768 | tf_op jit(solution)/shard_map/ppermute | solution.py:369
  10.0 0.8 collective-permute-start.1
  10.7 0.7 copy-done
  11.4 0.7 copy-done.1
  12.1 3.5 %order.1 = (s32[320,2]{1,0:T(8,128)S(1)}, f32[320,2]{1,0:T(8,128)S(1)}, bf16[2,2,1536,512]{3,2,1,0:T(8,128)(2,1)S(1)}) custom-call(s32[3]{0:T(128)S(1)} %pad_add_fusion.where_ref, s32[2,320]{1,0:T(2,128)S(1)} %bitcast.35, bf16[2,320]{1,0:T(2,128)(2,1)S(1)} %bitcast.36, bf16[4,2,1536,512]{3,2,1,0:T(8,128)(2,1)} %bitcast.40), custom_call_target="tpu_custom_call" | custom-call | bytes 12582912 | tf_op jit(solution)/shard_map/order/pallas_call | solution.py:83
  15.6 1.2 %collective-permute-done.2 = bf16[40,1024]{1,0:T(8,128)(2,1)S(1)} collective-permute-done((bf16[40,1024]{1,0:T(8,128)(2,1)S(1)}, bf16[40,1024]{1,0:T(8,128)(2,1)S(1)}, u32[]{:S(2)}, u32[]{:S(2)}) %collective-permute-start.2) | collective-permute-done | bytes 81952 | tf_op jit(solution)/shard_map/ppermute | solution.py:369
  16.9 0.6 collective-permute-start.5
  17.5 2.7 %collective-permute-start.8 = (bf16[80,512]{1,0:T(8,128)(2,1)S(1)}, bf16[80,512]{1,0:T(8,128)(2,1)S(1)}, u32[]{:S(2)}, u32[]{:S(2)}) collective-permute-start(bf16[80,512]{1,0:T(8,128)(2,1)S(1)} %pad_maximum_fusion.3), channel_id=1, source_target_pairs={{0,24},{2,26},{4,28},{6,30},{8,16},{10,18},{12,20},{14,22},{16,8},... | collective-permute-start | bytes 245768 | tf_op jit(solution)/shard_map/ppermute | solution.py:369
  20.2 1.7 %collective-permute-start.6 = (bf16[80,512]{1,0:T(8,128)(2,1)S(1)}, bf16[80,512]{1,0:T(8,128)(2,1)S(1)}, u32[]{:S(2)}, u32[]{:S(2)}) collective-permute-start(bf16[80,512]{1,0:T(8,128)(2,1)S(1)} %pad_maximum_fusion.3), channel_id=1, source_target_pairs={{0,8},{2,10},{4,12},{6,14},{8,0},{10,2},{12,4},{14,6},{16,24},{18,... | collective-permute-start | bytes 245768 | tf_op jit(solution)/shard_map/ppermute | solution.py:369
  21.9 4.7 %fetch.3 = bf16[4,3072,512]{2,1,0:T(8,128)(2,1)S(1)} custom-call(bf16[4,1,3072,512]{3,2,1,0:T(8,128)(2,1)} %bitcast.44), custom_call_target="tpu_custom_call" | custom-call | bytes 25165824 | tf_op jit(solution)/shard_map/fetch/pallas_call | solution.py:47
  27.3 3.4 %gate_gemm.2 = (f32[2,320,512]{2,1,0:T(8,128)S(1)}, bf16[2,2,1536,512]{3,2,1,0:T(8,128)(2,1)S(1)}) custom-call(s32[3]{0:T(128)S(1)} %pad_add_fusion.where_ref, s32[320,2]{1,0:T(8,128)S(1)} %get-tuple-element.45.ids_ref, bf16[320,1536]{1,0:T(8,128)(2,1)S(1)} %pad_maximum_fusion.rows_ref.own_ref, bf16[4,2,1536,512]{3,2,1,0:T(8,128)(2,1)S(1)} %bitcast.33, ...), custom_call_target="tpu_custom_call" | custom-call | flops 2013265920 | bytes 6291456 | tf_op jit(solution)/shard_map/gate_gemm/pallas_call | solution.py:155
  30.7 3.4 %gate_gemm.3 = (f32[2,160,512]{2,1,0:T(8,128)S(1)}, bf16[1,2,160,512]{3,2,1,0:T(8,128)(2,1)S(1)}) custom-call(s32[3]{0:T(128)S(1)} %pad_add_fusion.where_ref, s32[320,2]{1,0:T(8,128)S(1)} %get-tuple-element.45.ids_ref, bf16[320,1536]{1,0:T(8,128)(2,1)S(1)} %collective-permute-done.9.rows_ref.other_ref, bf16[4,2,1536,512]{3,2,1,0:T(8,128)(2,1)S(1)} %bitcast.34, ...), custom_call_target="tpu_custom_call" | custom-call | flops 2013265920 | bytes 6291456 | tf_op jit(solution)/shard_map/gate_gemm/pallas_call | solution.py:155
  34.1 1.6 %collective-permute-start.10 = (bf16[2,160,512]{2,1,0:T(8,128)(2,1)S(1)}, bf16[2,160,512]{2,1,0:T(8,128)(2,1)S(1)}, u32[]{:S(2)}, u32[]{:S(2)}) collective-permute-start(bf16[2,160,512]{2,1,0:T(8,128)(2,1)S(1)} %bitcast.37), channel_id=1, source_target_pairs={{0,1},{1,0},{2,3},{3,2},{4,5},{5,4},{6,7},{7,6},{8,9},{9,8},{10,11... | collective-permute-start | bytes 983048 | tf_op jit(solution)/shard_map/ppermute | solution.py:381
  35.7 2.8 %up_gemm.3 = (f32[2,160,256]{2,1,0:T(8,128)S(1)}, bf16[1,2,160,256]{3,2,1,0:T(8,128)(2,1)S(1)}) custom-call(s32[3]{0:T(128)S(1)} %pad_add_fusion.where_ref, s32[320,2]{1,0:T(8,128)S(1)} %get-tuple-element.45.ids_ref, bf16[320,1536]{1,0:T(8,128)(2,1)S(1)} %pad_maximum_fusion.rows_ref.own_ref, bf16[320,1536]{1,0:T(8,128)(2,1)S(1)} %collective-permute-done.9.rows_ref.other_ref, ...), custom_call_target="tpu_custom_call" | custom-call | flops 2013265920 | bytes 6291456 | tf_op jit(solution)/shard_map/up_gemm/pallas_call | solution.py:197
  38.6 0.5 collective-permute-start.12
  39.1 2.8 %up_gemm.2 = (f32[2,160,256]{2,1,0:T(8,128)S(1)}, bf16[1,2,160,256]{3,2,1,0:T(8,128)(2,1)S(1)}) custom-call(s32[3]{0:T(128)S(1)} %pad_add_fusion.where_ref, s32[320,2]{1,0:T(8,128)S(1)} %get-tuple-element.45.ids_ref, bf16[320,1536]{1,0:T(8,128)(2,1)S(1)} %pad_maximum_fusion.rows_ref.own_ref, bf16[320,1536]{1,0:T(8,128)(2,1)S(1)} %collective-permute-done.9.rows_ref.other_ref, ...), custom_call_target="tpu_custom_call" | custom-call | flops 2013265920 | bytes 6291456 | tf_op jit(solution)/shard_map/up_gemm/pallas_call | solution.py:197
  41.9 1.6 %collective-permute-start.11 = (bf16[2,160,256]{2,1,0:T(8,128)(2,1)S(1)}, bf16[2,160,256]{2,1,0:T(8,128)(2,1)S(1)}, u32[]{:S(2)}, u32[]{:S(2)}) collective-permute-start(bf16[2,160,256]{2,1,0:T(8,128)(2,1)S(1)} %bitcast.38), channel_id=1, source_target_pairs={{0,1},{1,0},{2,3},{3,2},{4,5},{5,4},{6,7},{7,6},{8,9},{9,8},{10,11... | collective-permute-start | bytes 491528 | tf_op jit(solution)/shard_map/ppermute | solution.py:381
  43.5 2.9 %fetch.4.refs_2_ = bf16[4,256,3072]{2,1,0:T(8,128)(2,1)S(1)} custom-call(bf16[4,2,256,3072]{3,2,1,0:T(8,128)(2,1)} %bitcast.42), custom_call_target="tpu_custom_call" | custom-call | bytes 12582912 | tf_op jit(solution)/shard_map/fetch/pallas_call | solution.py:47
  46.4 1.8 %collective-permute-done.12 = bf16[2,160,256]{2,1,0:T(8,128)(2,1)S(1)} collective-permute-done((bf16[2,160,256]{2,1,0:T(8,128)(2,1)S(1)}, bf16[2,160,256]{2,1,0:T(8,128)(2,1)S(1)}, u32[]{:S(2)}, u32[]{:S(2)}) %collective-permute-start.12) | collective-permute-done | bytes 163872 | tf_op jit(solution)/shard_map/ppermute | solution.py:381
  48.4 2.9 %fetch.5.wd_ref = bf16[4,256,3072]{2,1,0:T(8,128)(2,1)S(1)} custom-call(bf16[4,2,256,3072]{3,2,1,0:T(8,128)(2,1)} %bitcast.43), custom_call_target="tpu_custom_call" | custom-call | bytes 12582912 | tf_op jit(solution)/shard_map/fetch/pallas_call | solution.py:47
  51.4 1.6 %collective-permute-start.13 = (bf16[2,160,256]{2,1,0:T(8,128)(2,1)S(1)}, bf16[2,160,256]{2,1,0:T(8,128)(2,1)S(1)}, u32[]{:S(2)}, u32[]{:S(2)}) collective-permute-start(bf16[2,160,256]{2,1,0:T(8,128)(2,1)S(1)} %multiply_convert_fusion.refs_0_), channel_id=1, source_target_pairs={{0,1},{1,0},{2,3},{3,2},{4,5},{5,4},{6,7},{7,6},{8,9},{9,8},{10,11... | collective-permute-start | bytes 491528 | tf_op jit(solution)/shard_map/ppermute | solution.py:381
  53.5 5.0 %collective-permute-done.13.refs_1_ = bf16[2,160,256]{2,1,0:T(8,128)(2,1)S(1)} collective-permute-done((bf16[2,160,256]{2,1,0:T(8,128)(2,1)S(1)}, bf16[2,160,256]{2,1,0:T(8,128)(2,1)S(1)}, u32[]{:S(2)}, u32[]{:S(2)}) %collective-permute-start.13) | collective-permute-done | bytes 163872 | tf_op jit(solution)/shard_map/ppermute | solution.py:381
  58.6 1.0 %pick.1.rows_ref = bf16[4,320,256]{2,1,0:T(8,128)(2,1)S(1)} custom-call(s32[3]{0:T(128)S(1)} %pad_add_fusion.where_ref, s32[320,2]{1,0:T(8,128)S(1)} %get-tuple-element.45.ids_ref, bf16[2,160,256]{2,1,0:T(8,128)(2,1)S(1)} %multiply_convert_fusion.refs_0_, bf16[2,160,256]{2,1,0:T(8,128)(2,1)S(1)} %collective-permute-done.13.refs_1_), custom_call_target="tpu_custom_call" | custom-call | tf_op jit(solution)/shard_map/pick/pallas_call | solution.py:241
  59.5 1.2 %collective-permute-done.14.refs_1_ = bf16[2,160,256]{2,1,0:T(8,128)(2,1)S(1)} collective-permute-done((bf16[2,160,256]{2,1,0:T(8,128)(2,1)S(1)}, bf16[2,160,256]{2,1,0:T(8,128)(2,1)S(1)}, u32[]{:S(2)}, u32[]{:S(2)}) %collective-permute-start.14) | collective-permute-done | bytes 163872 | tf_op jit(solution)/shard_map/ppermute | solution.py:381
  60.7 3.6 %first_down.1.refs_0_ = f32[2,320,1536]{2,1,0:T(8,128)S(1)} custom-call(s32[3]{0:T(128)S(1)} %pad_add_fusion.where_ref, s32[320,2]{1,0:T(8,128)S(1)} %get-tuple-element.45.ids_ref, f32[320,2]{1,0:T(8,128)S(1)} %get-tuple-element.46.probs_ref, bf16[2,160,256]{2,1,0:T(8,128)(2,1)S(1)} %multiply_convert_fusion.1.refs_0_, ...), custom_call_target="tpu_custom_call" | custom-call | flops 2013265920 | bytes 6291456 | tf_op jit(solution)/shard_map/first_down/pallas_call | solution.py:274
  64.3 1.5 %down_other.2 = f32[320,768]{1,0:T(8,128)S(1)} custom-call(s32[3]{0:T(128)S(1)} %pad_add_fusion.where_ref, s32[320,2]{1,0:T(8,128)S(1)} %get-tuple-element.45.ids_ref, f32[320,2]{1,0:T(8,128)S(1)} %get-tuple-element.46.probs_ref, bf16[4,320,256]{2,1,0:T(8,128)(2,1)S(1)} %pick.1.rows_ref, bf16[4,256,3072]{2,1,0:T(8,128)(2,1)S(1)} %fetch.5.wd_ref, ...), custom_call_target="tpu_custom_call" | custom-call | flops 503316480 | bytes 1572864 | tf_op jit(solution)/shard_map/down_other/pallas_call | solution.py:316
  65.9 1.4 %down_other.3 = f32[320,768]{1,0:T(8,128)S(1)} custom-call(s32[3]{0:T(128)S(1)} %pad_add_fusion.where_ref, s32[320,2]{1,0:T(8,128)S(1)} %get-tuple-element.45.ids_ref, f32[320,2]{1,0:T(8,128)S(1)} %get-tuple-element.46.probs_ref, bf16[4,320,256]{2,1,0:T(8,128)(2,1)S(1)} %pick.1.rows_ref, bf16[4,256,3072]{2,1,0:T(8,128)(2,1)S(1)} %fetch.5.wd_ref, ...), custom_call_target="tpu_custom_call" | custom-call | flops 503316480 | bytes 1572864 | tf_op jit(solution)/shard_map/down_other/pallas_call | solution.py:316
  67.3 0.6 collective-permute-start.20
  67.9 1.5 %down_own.2 = f32[320,768]{1,0:T(8,128)S(1)} custom-call(s32[3]{0:T(128)S(1)} %pad_add_fusion.where_ref, s32[320,2]{1,0:T(8,128)S(1)} %get-tuple-element.45.ids_ref, f32[320,2]{1,0:T(8,128)S(1)} %get-tuple-element.46.probs_ref, bf16[4,320,256]{2,1,0:T(8,128)(2,1)S(1)} %pick.1.rows_ref, bf16[4,256,3072]{2,1,0:T(8,128)(2,1)S(1)} %fetch.5.wd_ref, ...), custom_call_target="tpu_custom_call" | custom-call | flops 503316480 | bytes 1572864 | tf_op jit(solution)/shard_map/down_own/pallas_call | solution.py:316
  69.5 1.5 %down_own.3 = f32[320,768]{1,0:T(8,128)S(1)} custom-call(s32[3]{0:T(128)S(1)} %pad_add_fusion.where_ref, s32[320,2]{1,0:T(8,128)S(1)} %get-tuple-element.45.ids_ref, f32[320,2]{1,0:T(8,128)S(1)} %get-tuple-element.46.probs_ref, bf16[4,320,256]{2,1,0:T(8,128)(2,1)S(1)} %pick.1.rows_ref, bf16[4,256,3072]{2,1,0:T(8,128)(2,1)S(1)} %fetch.5.wd_ref, ...), custom_call_target="tpu_custom_call" | custom-call | flops 503316480 | bytes 1572864 | tf_op jit(solution)/shard_map/down_own/pallas_call | solution.py:316
  71.2 1.6 %collective-permute-start.21 = (bf16[4,40,768]{2,1,0:T(8,128)(2,1)S(1)}, bf16[4,40,768]{2,1,0:T(8,128)(2,1)S(1)}, u32[]{:S(2)}, u32[]{:S(2)}) collective-permute-start(bf16[4,40,768]{2,1,0:T(8,128)(2,1)S(1)} %bitcast.48), channel_id=1, source_target_pairs={{0,4},{2,6},{4,0},{6,2},{8,12},{10,14},{12,8},{14,10},{16,20},{18,... | collective-permute-start | bytes 737288 | tf_op jit(solution)/shard_map/ppermute | solution.py:369
  72.9 0.5 collective-permute-start.16
  73.5 6.6 %collective-permute-done.21 = bf16[4,40,768]{2,1,0:T(8,128)(2,1)S(1)} collective-permute-done((bf16[4,40,768]{2,1,0:T(8,128)(2,1)S(1)}, bf16[4,40,768]{2,1,0:T(8,128)(2,1)S(1)}, u32[]{:S(2)}, u32[]{:S(2)}) %collective-permute-start.21) | collective-permute-done | bytes 245792 | tf_op jit(solution)/shard_map/ppermute | solution.py:369
  80.2 2.3 %collective-permute-start.24 = (bf16[40,768]{1,0:T(8,128)(2,1)S(1)}, bf16[40,768]{1,0:T(8,128)(2,1)S(1)}, u32[]{:S(2)}, u32[]{:S(2)}) collective-permute-start(bf16[40,768]{1,0:T(8,128)(2,1)S(1)} %get-tuple-element.85), channel_id=1, source_target_pairs={{0,24},{2,26},{4,28},{6,30},{8,16},{10,18},{12,20},{14,22},{16,8},... | collective-permute-start | bytes 184328 | tf_op jit(solution)/shard_map/ppermute | solution.py:369
  82.6 1.1 %collective-permute-start.23 = (bf16[40,768]{1,0:T(8,128)(2,1)S(1)}, bf16[40,768]{1,0:T(8,128)(2,1)S(1)}, u32[]{:S(2)}, u32[]{:S(2)}) collective-permute-start(bf16[40,768]{1,0:T(8,128)(2,1)S(1)} %get-tuple-element.86), channel_id=1, source_target_pairs={{0,16},{2,18},{4,20},{6,22},{8,24},{10,26},{12,28},{14,30},{16,0},... | collective-permute-start | bytes 184328 | tf_op jit(solution)/shard_map/ppermute | solution.py:369
  83.7 0.7 collective-permute-done.16
  84.8 2.3 %collective-permute-start.19 = (bf16[40,768]{1,0:T(8,128)(2,1)S(1)}, bf16[40,768]{1,0:T(8,128)(2,1)S(1)}, u32[]{:S(2)}, u32[]{:S(2)}) collective-permute-start(bf16[40,768]{1,0:T(8,128)(2,1)S(1)} %get-tuple-element.82), channel_id=1, source_target_pairs={{0,24},{2,26},{4,28},{6,30},{8,16},{10,18},{12,20},{14,22},{16,8},... | collective-permute-start | bytes 184328 | tf_op jit(solution)/shard_map/ppermute | solution.py:369
  87.2 1.0 %collective-permute-start.18 = (bf16[40,768]{1,0:T(8,128)(2,1)S(1)}, bf16[40,768]{1,0:T(8,128)(2,1)S(1)}, u32[]{:S(2)}, u32[]{:S(2)}) collective-permute-start(bf16[40,768]{1,0:T(8,128)(2,1)S(1)} %get-tuple-element.83), channel_id=1, source_target_pairs={{0,16},{2,18},{4,20},{6,22},{8,24},{10,26},{12,28},{14,30},{16,0},... | collective-permute-start | bytes 184328 | tf_op jit(solution)/shard_map/ppermute | solution.py:369
  88.2 1.1 %collective-permute-done.23 = bf16[40,768]{1,0:T(8,128)(2,1)S(1)} collective-permute-done((bf16[40,768]{1,0:T(8,128)(2,1)S(1)}, bf16[40,768]{1,0:T(8,128)(2,1)S(1)}, u32[]{:S(2)}, u32[]{:S(2)}) %collective-permute-start.23) | collective-permute-done | bytes 61472 | tf_op jit(solution)/shard_map/ppermute | solution.py:369
  89.6 1.4 %collective-permute-done.19 = bf16[40,768]{1,0:T(8,128)(2,1)S(1)} collective-permute-done((bf16[40,768]{1,0:T(8,128)(2,1)S(1)}, bf16[40,768]{1,0:T(8,128)(2,1)S(1)}, u32[]{:S(2)}, u32[]{:S(2)}) %collective-permute-start.19) | collective-permute-done | bytes 61472 | tf_op jit(solution)/shard_map/ppermute | solution.py:369
  91.0 2.6 %collective-permute-done.18 = bf16[40,768]{1,0:T(8,128)(2,1)S(1)} collective-permute-done((bf16[40,768]{1,0:T(8,128)(2,1)S(1)}, bf16[40,768]{1,0:T(8,128)(2,1)S(1)}, u32[]{:S(2)}, u32[]{:S(2)}) %collective-permute-start.18) | collective-permute-done | bytes 61472 | tf_op jit(solution)/shard_map/ppermute | solution.py:369
  93.8 1.3 %collective-permute-done.25 = bf16[20,1536]{1,0:T(8,128)(2,1)S(1)} collective-permute-done((bf16[20,1536]{1,0:T(8,128)(2,1)S(1)}, bf16[20,1536]{1,0:T(8,128)(2,1)S(1)}, u32[]{:S(2)}, u32[]{:S(2)}) %collective-permute-start.25) | collective-permute-done | bytes 61472 | tf_op jit(solution)/shard_map/ppermute | solution.py:369
  95.1 0.7 pad_maximum_fusion.2
  (61 shorter events, 3.1 us)
Async XLA Ops:
  0.9 1.5 %collective-permute-start = (bf16[20,1536]{1,0:T(8,128)(2,1)S(1)}, bf16[20,1536]{1,0:T(8,128)(2,1)S(1)}, u32[]{:S(2)}, u32[]{:S(2)}) collective-permute-start(bf16[20,1536]{1,0:T(8,128)(2,1)S(1)} %broadcast_select_fusion.6), channel_id=1, source_target_pairs={{0,2},{2,0},{4,6},{6,4},{8,10},{10,8},{12,14},{14,12},{16,18},{18,... | collective-permute-start | bytes 184328 | tf_op jit(solution)/shard_map/ppermute | solution.py:369
  3.4 12.2 %collective-permute-start.4 = (bf16[40,512]{1,0:T(8,128)(2,1)S(1)}, bf16[40,512]{1,0:T(8,128)(2,1)S(1)}, u32[]{:S(2)}, u32[]{:S(2)}) collective-permute-start(bf16[40,512]{1,0:T(8,128)(2,1)S(1)} %pad_maximum_fusion.5), channel_id=1, source_target_pairs={{0,4},{2,6},{4,0},{6,2},{8,12},{10,14},{12,8},{14,10},{16,20},{18,... | collective-permute-start | bytes 122888 | tf_op jit(solution)/shard_map/ppermute | solution.py:369
  6.3 9.3 %collective-permute-start.3 = (bf16[40,1024]{1,0:T(8,128)(2,1)S(1)}, bf16[40,1024]{1,0:T(8,128)(2,1)S(1)}, u32[]{:S(2)}, u32[]{:S(2)}) collective-permute-start(bf16[40,1024]{1,0:T(8,128)(2,1)S(1)} %fusion), channel_id=1, source_target_pairs={{0,24},{2,26},{4,28},{6,30},{8,16},{10,18},{12,20},{14,22},{16,8},... | collective-permute-start | bytes 245768 | tf_op jit(solution)/shard_map/ppermute | solution.py:369
  9.9 6.9 %collective-permute-start.2 = (bf16[40,1024]{1,0:T(8,128)(2,1)S(1)}, bf16[40,1024]{1,0:T(8,128)(2,1)S(1)}, u32[]{:S(2)}, u32[]{:S(2)}) collective-permute-start(bf16[40,1024]{1,0:T(8,128)(2,1)S(1)} %fusion), channel_id=1, source_target_pairs={{0,16},{2,18},{4,20},{6,22},{8,24},{10,26},{12,28},{14,30},{16,0},... | collective-permute-start | bytes 245768 | tf_op jit(solution)/shard_map/ppermute | solution.py:369
  10.0 6.9 %collective-permute-start.1 = (bf16[40,1024]{1,0:T(8,128)(2,1)S(1)}, bf16[40,1024]{1,0:T(8,128)(2,1)S(1)}, u32[]{:S(2)}, u32[]{:S(2)}) collective-permute-start(bf16[40,1024]{1,0:T(8,128)(2,1)S(1)} %fusion), channel_id=1, source_target_pairs={{0,8},{2,10},{4,12},{6,14},{8,0},{10,2},{12,4},{14,6},{16,24},{18,... | collective-permute-start | bytes 245768 | tf_op jit(solution)/shard_map/ppermute | solution.py:369
  10.7 0.7 copy-start
  11.4 0.7 copy-start.1
  16.9 10.2 %collective-permute-start.5 = (bf16[160,1024]{1,0:T(8,128)(2,1)S(1)}, bf16[160,1024]{1,0:T(8,128)(2,1)S(1)}, u32[]{:S(2)}, u32[]{:S(2)}) collective-permute-start(bf16[160,1024]{1,0:T(8,128)(2,1)S(1)} %pad_maximum_fusion.1), channel_id=1, source_target_pairs={{0,4},{2,6},{4,0},{6,2},{8,12},{10,14},{12,8},{14,10},{16,20},{18,... | collective-permute-start | bytes 983048 | tf_op jit(solution)/shard_map/ppermute | solution.py:369
  17.5 9.1 %collective-permute-start.8 = (bf16[80,512]{1,0:T(8,128)(2,1)S(1)}, bf16[80,512]{1,0:T(8,128)(2,1)S(1)}, u32[]{:S(2)}, u32[]{:S(2)}) collective-permute-start(bf16[80,512]{1,0:T(8,128)(2,1)S(1)} %pad_maximum_fusion.3), channel_id=1, source_target_pairs={{0,24},{2,26},{4,28},{6,30},{8,16},{10,18},{12,20},{14,22},{16,8},... | collective-permute-start | bytes 245768 | tf_op jit(solution)/shard_map/ppermute | solution.py:369
  20.2 6.9 %collective-permute-start.7 = (bf16[80,512]{1,0:T(8,128)(2,1)S(1)}, bf16[80,512]{1,0:T(8,128)(2,1)S(1)}, u32[]{:S(2)}, u32[]{:S(2)}) collective-permute-start(bf16[80,512]{1,0:T(8,128)(2,1)S(1)} %pad_maximum_fusion.3), channel_id=1, source_target_pairs={{0,16},{2,18},{4,20},{6,22},{8,24},{10,26},{12,28},{14,30},{16,0},... | collective-permute-start | bytes 245768 | tf_op jit(solution)/shard_map/ppermute | solution.py:369
  20.2 6.9 %collective-permute-start.6 = (bf16[80,512]{1,0:T(8,128)(2,1)S(1)}, bf16[80,512]{1,0:T(8,128)(2,1)S(1)}, u32[]{:S(2)}, u32[]{:S(2)}) collective-permute-start(bf16[80,512]{1,0:T(8,128)(2,1)S(1)} %pad_maximum_fusion.3), channel_id=1, source_target_pairs={{0,8},{2,10},{4,12},{6,14},{8,0},{10,2},{12,4},{14,6},{16,24},{18,... | collective-permute-start | bytes 245768 | tf_op jit(solution)/shard_map/ppermute | solution.py:369
  27.2 3.5 %collective-permute-start.9 = (bf16[320,1536]{1,0:T(8,128)(2,1)S(1)}, bf16[320,1536]{1,0:T(8,128)(2,1)S(1)}, u32[]{:S(2)}, u32[]{:S(2)}) collective-permute-start(bf16[320,1536]{1,0:T(8,128)(2,1)S(1)} %pad_maximum_fusion.rows_ref.own_ref), channel_id=1, source_target_pairs={{0,2},{2,0},{4,6},{6,4},{8,10},{10,8},{12,14},{14,12},{16,18},{18,... | collective-permute-start | bytes 2949128 | tf_op jit(solution)/shard_map/ppermute | solution.py:369
  34.1 14.2 %collective-permute-start.10 = (bf16[2,160,512]{2,1,0:T(8,128)(2,1)S(1)}, bf16[2,160,512]{2,1,0:T(8,128)(2,1)S(1)}, u32[]{:S(2)}, u32[]{:S(2)}) collective-permute-start(bf16[2,160,512]{2,1,0:T(8,128)(2,1)S(1)} %bitcast.37), channel_id=1, source_target_pairs={{0,1},{1,0},{2,3},{3,2},{4,5},{5,4},{6,7},{7,6},{8,9},{9,8},{10,11... | collective-permute-start | bytes 983048 | tf_op jit(solution)/shard_map/ppermute | solution.py:381
  38.6 9.7 %collective-permute-start.12 = (bf16[2,160,256]{2,1,0:T(8,128)(2,1)S(1)}, bf16[2,160,256]{2,1,0:T(8,128)(2,1)S(1)}, u32[]{:S(2)}, u32[]{:S(2)}) collective-permute-start(bf16[2,160,256]{2,1,0:T(8,128)(2,1)S(1)} %bitcast.39), channel_id=1, source_target_pairs={{0,1},{1,0},{2,3},{3,2},{4,5},{5,4},{6,7},{7,6},{8,9},{9,8},{10,11... | collective-permute-start | bytes 491528 | tf_op jit(solution)/shard_map/ppermute | solution.py:381
  41.9 9.4 %collective-permute-start.11 = (bf16[2,160,256]{2,1,0:T(8,128)(2,1)S(1)}, bf16[2,160,256]{2,1,0:T(8,128)(2,1)S(1)}, u32[]{:S(2)}, u32[]{:S(2)}) collective-permute-start(bf16[2,160,256]{2,1,0:T(8,128)(2,1)S(1)} %bitcast.38), channel_id=1, source_target_pairs={{0,1},{1,0},{2,3},{3,2},{4,5},{5,4},{6,7},{7,6},{8,9},{9,8},{10,11... | collective-permute-start | bytes 491528 | tf_op jit(solution)/shard_map/ppermute | solution.py:381
  51.4 7.1 %collective-permute-start.13 = (bf16[2,160,256]{2,1,0:T(8,128)(2,1)S(1)}, bf16[2,160,256]{2,1,0:T(8,128)(2,1)S(1)}, u32[]{:S(2)}, u32[]{:S(2)}) collective-permute-start(bf16[2,160,256]{2,1,0:T(8,128)(2,1)S(1)} %multiply_convert_fusion.refs_0_), channel_id=1, source_target_pairs={{0,1},{1,0},{2,3},{3,2},{4,5},{5,4},{6,7},{7,6},{8,9},{9,8},{10,11... | collective-permute-start | bytes 491528 | tf_op jit(solution)/shard_map/ppermute | solution.py:381
  53.1 7.7 %collective-permute-start.14 = (bf16[2,160,256]{2,1,0:T(8,128)(2,1)S(1)}, bf16[2,160,256]{2,1,0:T(8,128)(2,1)S(1)}, u32[]{:S(2)}, u32[]{:S(2)}) collective-permute-start(bf16[2,160,256]{2,1,0:T(8,128)(2,1)S(1)} %multiply_convert_fusion.1.refs_0_), channel_id=1, source_target_pairs={{0,1},{1,0},{2,3},{3,2},{4,5},{5,4},{6,7},{7,6},{8,9},{9,8},{10,11... | collective-permute-start | bytes 491528 | tf_op jit(solution)/shard_map/ppermute | solution.py:381
  65.8 3.6 %collective-permute-start.15 = (f32[320,768]{1,0:T(8,128)S(1)}, f32[320,768]{1,0:T(8,128)S(1)}, u32[]{:S(2)}, u32[]{:S(2)}) collective-permute-start(f32[320,768]{1,0:T(8,128)S(1)} %down_other.2), channel_id=1, source_target_pairs={{0,2},{2,0},{4,6},{6,4},{8,10},{10,8},{12,14},{14,12},{16,18},{18,... | collective-permute-start | bytes 2949128 | tf_op jit(solution)/shard_map/ppermute | solution.py:369
  67.3 3.7 %collective-permute-start.20 = (f32[320,768]{1,0:T(8,128)S(1)}, f32[320,768]{1,0:T(8,128)S(1)}, u32[]{:S(2)}, u32[]{:S(2)}) collective-permute-start(f32[320,768]{1,0:T(8,128)S(1)} %down_other.3), channel_id=1, source_target_pairs={{0,2},{2,0},{4,6},{6,4},{8,10},{10,8},{12,14},{14,12},{16,18},{18,... | collective-permute-start | bytes 2949128 | tf_op jit(solution)/shard_map/ppermute | solution.py:369
  71.2 8.9 %collective-permute-start.21 = (bf16[4,40,768]{2,1,0:T(8,128)(2,1)S(1)}, bf16[4,40,768]{2,1,0:T(8,128)(2,1)S(1)}, u32[]{:S(2)}, u32[]{:S(2)}) collective-permute-start(bf16[4,40,768]{2,1,0:T(8,128)(2,1)S(1)} %bitcast.48), channel_id=1, source_target_pairs={{0,4},{2,6},{4,0},{6,2},{8,12},{10,14},{12,8},{14,10},{16,20},{18,... | collective-permute-start | bytes 737288 | tf_op jit(solution)/shard_map/ppermute | solution.py:369
  72.9 11.5 %collective-permute-start.16 = (bf16[4,40,768]{2,1,0:T(8,128)(2,1)S(1)}, bf16[4,40,768]{2,1,0:T(8,128)(2,1)S(1)}, u32[]{:S(2)}, u32[]{:S(2)}) collective-permute-start(bf16[4,40,768]{2,1,0:T(8,128)(2,1)S(1)} %bitcast.47), channel_id=1, source_target_pairs={{0,4},{2,6},{4,0},{6,2},{8,12},{10,14},{12,8},{14,10},{16,20},{18,... | collective-permute-start | bytes 737288 | tf_op jit(solution)/shard_map/ppermute | solution.py:369
  80.2 7.0 %collective-permute-start.22 = (bf16[40,768]{1,0:T(8,128)(2,1)S(1)}, bf16[40,768]{1,0:T(8,128)(2,1)S(1)}, u32[]{:S(2)}, u32[]{:S(2)}) collective-permute-start(bf16[40,768]{1,0:T(8,128)(2,1)S(1)} %get-tuple-element.84), channel_id=1, source_target_pairs={{0,8},{2,10},{4,12},{6,14},{8,0},{10,2},{12,4},{14,6},{16,24},{18,... | collective-permute-start | bytes 184328 | tf_op jit(solution)/shard_map/ppermute | solution.py:369
  80.2 7.9 %collective-permute-start.24 = (bf16[40,768]{1,0:T(8,128)(2,1)S(1)}, bf16[40,768]{1,0:T(8,128)(2,1)S(1)}, u32[]{:S(2)}, u32[]{:S(2)}) collective-permute-start(bf16[40,768]{1,0:T(8,128)(2,1)S(1)} %get-tuple-element.85), channel_id=1, source_target_pairs={{0,24},{2,26},{4,28},{6,30},{8,16},{10,18},{12,20},{14,22},{16,8},... | collective-permute-start | bytes 184328 | tf_op jit(solution)/shard_map/ppermute | solution.py:369
  82.6 6.7 %collective-permute-start.23 = (bf16[40,768]{1,0:T(8,128)(2,1)S(1)}, bf16[40,768]{1,0:T(8,128)(2,1)S(1)}, u32[]{:S(2)}, u32[]{:S(2)}) collective-permute-start(bf16[40,768]{1,0:T(8,128)(2,1)S(1)} %get-tuple-element.86), channel_id=1, source_target_pairs={{0,16},{2,18},{4,20},{6,22},{8,24},{10,26},{12,28},{14,30},{16,0},... | collective-permute-start | bytes 184328 | tf_op jit(solution)/shard_map/ppermute | solution.py:369
  84.5 5.1 %collective-permute-start.17 = (bf16[40,768]{1,0:T(8,128)(2,1)S(1)}, bf16[40,768]{1,0:T(8,128)(2,1)S(1)}, u32[]{:S(2)}, u32[]{:S(2)}) collective-permute-start(bf16[40,768]{1,0:T(8,128)(2,1)S(1)} %get-tuple-element.81), channel_id=1, source_target_pairs={{0,8},{2,10},{4,12},{6,14},{8,0},{10,2},{12,4},{14,6},{16,24},{18,... | collective-permute-start | bytes 184328 | tf_op jit(solution)/shard_map/ppermute | solution.py:369
  84.8 6.2 %collective-permute-start.19 = (bf16[40,768]{1,0:T(8,128)(2,1)S(1)}, bf16[40,768]{1,0:T(8,128)(2,1)S(1)}, u32[]{:S(2)}, u32[]{:S(2)}) collective-permute-start(bf16[40,768]{1,0:T(8,128)(2,1)S(1)} %get-tuple-element.82), channel_id=1, source_target_pairs={{0,24},{2,26},{4,28},{6,30},{8,16},{10,18},{12,20},{14,22},{16,8},... | collective-permute-start | bytes 184328 | tf_op jit(solution)/shard_map/ppermute | solution.py:369
  87.2 6.4 %collective-permute-start.18 = (bf16[40,768]{1,0:T(8,128)(2,1)S(1)}, bf16[40,768]{1,0:T(8,128)(2,1)S(1)}, u32[]{:S(2)}, u32[]{:S(2)}) collective-permute-start(bf16[40,768]{1,0:T(8,128)(2,1)S(1)} %get-tuple-element.83), channel_id=1, source_target_pairs={{0,16},{2,18},{4,20},{6,22},{8,24},{10,26},{12,28},{14,30},{16,0},... | collective-permute-start | bytes 184328 | tf_op jit(solution)/shard_map/ppermute | solution.py:369
  93.7 1.3 %collective-permute-start.25 = (bf16[20,1536]{1,0:T(8,128)(2,1)S(1)}, bf16[20,1536]{1,0:T(8,128)(2,1)S(1)}, u32[]{:S(2)}, u32[]{:S(2)}) collective-permute-start(bf16[20,1536]{1,0:T(8,128)(2,1)S(1)} %broadcast_select_fusion.2), channel_id=1, source_target_pairs={{0,2},{2,0},{4,6},{6,4},{8,10},{10,8},{12,14},{14,12},{16,18},{18,... | collective-permute-start | bytes 184328 | tf_op jit(solution)/shard_map/ppermute | solution.py:369
where the time goes:
time: 96 us; the launch traced here: 95.8 us
  Pallas kernels  36.7 us (38%)
  starting transfers between devices  28.9 us (30%)
  waiting for transfers between devices  24.6 us (26%)
  other arithmetic  3.52 us (4%)
  local copies, waits for them, and re-layouts  1.59 us (2%)
    ppermute x21, starting transfers between devices, flip(): return lax.ppermute(x, 'dp', [(i, i ^ bits) for i in range(members)])  23 us
    ppermute x21, waiting for transfers between devices, flip(): return lax.ppermute(x, 'dp', [(i, i ^ bits) for i in range(members)])  16.5 us
    pallas_call x3, Pallas kernels, fetch(): pl.pallas_call(functools.partial(fetch_kernel, part), in_specs=[pl.BlockS...  10.4 us
    ppermute x5, waiting for transfers between devices, over_tensor(): lax.ppermute(x[s - 1], 'tensor', [(i, (i + s) % n) for i in range(n)])  8.11 us
    pallas_call x2, Pallas kernels, gate_gemm(): pl.pallas_call(functools.partial(gate_kernel, n, stage), in_specs=[pl.Blo...  6.77 us
    ppermute x5, starting transfers between devices, over_tensor(): lax.ppermute(x[s - 1], 'tensor', [(i, (i + s) % n) for i in range(n)])  5.88 us
    pallas_call x4, Pallas kernels, last_down(): pl.pallas_call(functools.partial(last_kernel, own, begin), in_specs=[pl.B...  5.82 us
    pallas_call x2, Pallas kernels, up_gemm(): pl.pallas_call(functools.partial(up_kernel, n, part), in_specs=[pl.BlockS...  5.64 us
  transfers between devices with their start and end apart: 26, of which 13 were waited for; matrix products, arithmetic and copies ran while one was open for 1% of the time, Pallas kernels for 30%

commit v1 on v0

--- a/solution.py
+++ b/solution.py
@@ -56,10 +56,19 @@
     )(in_hbm(w))
 
 
-def order_kernel(lines, chip_rows, where_ref, ids_ref, probs_ref, wu_ref, ids_out, probs_out, fetched_ref, sem_ref):
+def order_kernel(lines, chip_rows, where_ref, ids_in, probs_in, wu_ref, ids_out, probs_out, fetched_ref, *scratch):
+    ids_ref, probs_ref, sem_ref, small_sem = scratch
+    small = [
+        pltpu.make_async_copy(ids_in, ids_ref, small_sem.at[0]),
+        pltpu.make_async_copy(probs_in, probs_ref, small_sem.at[1]),
+    ]
+    for copy in small:
+        copy.start()
     copies = copies_of(lambda e: wu_ref.at[e], fetched_ref, sem_ref)
     for copy in copies:
         copy.start()
+    for copy in small:
+        copy.wait()
     top, token_count = ids_ref.shape
     row = lax.broadcasted_iota(jnp.int32, (chip_rows, token_count), 0)
     column = lax.broadcasted_iota(jnp.int32, (chip_rows, token_count), 1)
@@ -82,18 +91,23 @@
     inside = pl.BlockSpec(memory_space=pltpu.VMEM)
     return pl.pallas_call(
         functools.partial(order_kernel, lines, chip_rows),
-        in_specs=[pl.BlockSpec(memory_space=pltpu.SMEM), inside, inside, pl.BlockSpec(memory_space=pltpu.HBM)],
+        in_specs=[pl.BlockSpec(memory_space=pltpu.SMEM)] + [pl.BlockSpec(memory_space=pltpu.HBM)] * 3,
         out_specs=[inside] * 3,
         out_shape=[
             jax.ShapeDtypeStruct((token_count, top), jnp.int32),
             jax.ShapeDtypeStruct((token_count, top), F32),
             pltpu.VMEM((count,) + w_up.shape[1:], w_up.dtype),
         ],
-        scratch_shapes=[pltpu.SemaphoreType.DMA((count, 2))],
+        scratch_shapes=[
+            pltpu.VMEM((top, token_count), jnp.int32),
+            pltpu.VMEM((top, token_count), BF),
+            pltpu.SemaphoreType.DMA((count, 2)),
+            pltpu.SemaphoreType.DMA((2,)),
+        ],
         cost_estimate=pl.CostEstimate(flops=0, bytes_accessed=4 * w_up.size // 2, transcendentals=0),
         compiler_params=pltpu.CompilerParams(vmem_limit_bytes=LIMIT),
         name="order",
-    )(where, ids.T, probs.T, in_hbm(w_up))
+    )(where, in_hbm(ids.T), in_hbm(probs.T), in_hbm(w_up))
 
 
 def share_out(n, me, acc_ref, keep_ref, send_ref):
@@ -390,9 +404,10 @@
             keep = keep + part.astype(F32)
         return keep
 
-    left, right = tokens[:, :half], tokens[:, half:]
-    theirs = on_chip(jnp.where(first, right, left))
-    block = pair(jnp.where(first, left, right), theirs, 0)
+    theirs = on_chip(tokens)
+    upper = jnp.where(first, tokens[:, :half], theirs[:, half:])
+    lower = jnp.where(first, theirs[:, :half], tokens[:, half:])
+    block = jnp.concatenate([upper, lower], axis=0)
     near, far = block[:, :cut], block[:, cut:]
     near_line = [near] + [over_z(near, k) for k in range(1, lines)]
     far_other = over_x(far)
@@ -440,22 +455,19 @@
         downs = [first_down(n, where, ids, probs, hiddens[0], down_parts[0])]
     rows = pick(n, where, ids, hiddens[-1], experts)
     spans = ((0, middle), (middle, half))
-    away = []
+    kept, sent = [], []
     for begin, end in spans:
-        part = last_down(where, ids, probs, rows, down_parts[-1], downs, False, begin, end)
-        part, rows = lax.optimization_barrier((part, rows))
-        away.append(on_chip(part))
-    kept, sent = [], []
-    for i, (begin, end) in enumerate(spans):
+        shape = (2, lines, chip_rows, end - begin)
+        away = on_chip(last_down(where, ids, probs, rows, down_parts[-1], downs, False, begin, end))
         stay = last_down(where, ids, probs, rows, down_parts[-1], downs, True, begin, end)
-        total = (stay + away[i]).reshape(2, lines, chip_rows, end - begin)
-        part, rows = lax.optimization_barrier((total[1].astype(BF), rows))
-        kept.append(total[0])
+        away, stay = away.reshape(shape), stay.reshape(shape)
+        part, rows = lax.optimization_barrier(((stay[1] + away[1]).astype(BF), rows))
         sent.append(over_x(part))
+        kept.append(own_sum(stay[0], away[0]))
     outs = []
     for i in range(len(spans)):
-        line = kept[i] + sent[i].astype(F32)
-        arrived = [over_z(line[k].astype(BF), k) for k in range(1, lines)]
+        line = kept[i][1:] + sent[i][1:].astype(F32)
+        arrived = [over_z(line[k - 1].astype(BF), k) for k in range(1, lines)]
         mine = own_sum(kept[i][0], sent[i][0])
         outs.append(added(mine, arrived))
     mixed = jnp.concatenate(outs, axis=1).astype(BF)

time: 96 us -> 99.3 us (1.034)
  waiting for transfers between devices: 24.6 us -> 29.6 us
  local copies, waits for them, and re-layouts: 1.59 us -> 0.1 us
    ppermute x21, waiting for transfers between devices: 16.5 us -> 21.6 us  [flip(): return lax.ppermute(x, 'dp', [(i, i ^ bits) for i in range(members)])]
    unnamed x11 -> x7, local copies, waits for them, and re-layouts: 1.4 us -> 0.04 us
  transfers between devices with their start and end apart: 26 -> 26, of which waited for: 13 -> 15; matrix products, arithmetic and copies ran while one was open for 1% -> 1% of each run, Pallas kernels for 30% -> 27%
where the time goes in v1:
time: 99.3 us; the launch traced here: 99.1 us
  Pallas kernels  36.9 us (37%)
  waiting for transfers between devices  29.6 us (30%)
  starting transfers between devices  29.5 us (30%)
  other arithmetic  2.6 us (3%)
    ppermute x21, starting transfers between devices, flip(): return lax.ppermute(x, 'dp', [(i, i ^ bits) for i in range(members)])  23.6 us
    ppermute x21, waiting for transfers between devices, flip(): return lax.ppermute(x, 'dp', [(i, i ^ bits) for i in range(members)])  21.6 us
    pallas_call x3, Pallas kernels, fetch(): pl.pallas_call(functools.partial(fetch_kernel, part), in_specs=[pl.BlockS...  10.4 us
    ppermute x5, waiting for transfers between devices, over_tensor(): lax.ppermute(x[s - 1], 'tensor', [(i, (i + s) % n) for i in range(n)])  8.08 us
    pallas_call x2, Pallas kernels, gate_gemm(): pl.pallas_call(functools.partial(gate_kernel, n, stage), in_specs=[pl.Blo...  6.77 us
    pallas_call x4, Pallas kernels, last_down(): pl.pallas_call(functools.partial(last_kernel, own, begin), in_specs=[pl.B...  5.9 us
    ppermute x5, starting transfers between devices, over_tensor(): lax.ppermute(x[s - 1], 'tensor', [(i, (i + s) % n) for i in range(n)])  5.9 us
    pallas_call x2, Pallas kernels, up_gemm(): pl.pallas_call(functools.partial(up_kernel, n, part), in_specs=[pl.BlockS...  5.64 us
  transfers between devices with their start and end apart: 26, of which 15 were waited for; matrix products, arithmetic and copies ran while one was open for 1% of the time, Pallas kernels for 27%

profile of v1, /device:TPU:0, one launch (start us, length us, event | category | flops | bytes accessed | tf_op | source)
XLA Modules:
  0.0 99.1 jit_solution(6623054977105763874)
XLA Ops:
  0.0 0.5 collective-permute-start
  0.6 1.1 %collective-permute-done = bf16[20,3072]{1,0:T(8,128)(2,1)S(1)} collective-permute-done((bf16[20,3072]{1,0:T(8,128)(2,1)}, bf16[20,3072]{1,0:T(8,128)(2,1)S(1)}, u32[]{:S(2)}, u32[]{:S(2)}) %collective-permute-start) | collective-permute-done | bytes 122912 | tf_op jit(solution)/shard_map/ppermute | solution.py:383
  1.7 0.9 slice_select_fusion
  2.7 2.9 %collective-permute-start.4 = (bf16[40,512]{1,0:T(8,128)(2,1)S(1)}, bf16[40,512]{1,0:T(8,128)(2,1)S(1)}, u32[]{:S(2)}, u32[]{:S(2)}) collective-permute-start(bf16[40,512]{1,0:T(8,128)(2,1)S(1)} %pad_maximum_fusion.5), channel_id=1, source_target_pairs={{0,4},{2,6},{4,0},{6,2},{8,12},{10,14},{12,8},{14,10},{16,20},{18,... | collective-permute-start | bytes 122888 | tf_op jit(solution)/shard_map/ppermute | solution.py:383
  5.6 3.7 %collective-permute-start.3 = (bf16[40,1024]{1,0:T(8,128)(2,1)S(1)}, bf16[40,1024]{1,0:T(8,128)(2,1)S(1)}, u32[]{:S(2)}, u32[]{:S(2)}) collective-permute-start(bf16[40,1024]{1,0:T(8,128)(2,1)S(1)} %fusion.4), channel_id=1, source_target_pairs={{0,24},{2,26},{4,28},{6,30},{8,16},{10,18},{12,20},{14,22},{16,8},... | collective-permute-start | bytes 245768 | tf_op jit(solution)/shard_map/ppermute | solution.py:383
  9.3 0.8 collective-permute-start.1
  10.1 3.5 %order.1 = (s32[320,2]{1,0:T(8,128)S(1)}, f32[320,2]{1,0:T(8,128)S(1)}, bf16[2,2,1536,512]{3,2,1,0:T(8,128)(2,1)S(1)}) custom-call(s32[3]{0:T(128)S(1)} %pad_add_fusion.where_ref, s32[2,320]{1,0:T(2,128)} %bitcast.55, bf16[2,320]{1,0:T(2,128)(2,1)} %bitcast.56, bf16[4,2,1536,512]{3,2,1,0:T(8,128)(2,1)} %bitcast.48), custom_call_target="tpu_custom_call" | custom-call | bytes 12582912 | tf_op jit(solution)/shard_map/order/pallas_call | solution.py:92
  13.6 2.6 %collective-permute-done.2 = bf16[40,1024]{1,0:T(8,128)(2,1)S(1)} collective-permute-done((bf16[40,1024]{1,0:T(8,128)(2,1)S(1)}, bf16[40,1024]{1,0:T(8,128)(2,1)S(1)}, u32[]{:S(2)}, u32[]{:S(2)}) %collective-permute-start.2) | collective-permute-done | bytes 81952 | tf_op jit(solution)/shard_map/ppermute | solution.py:383
  16.2 0.6 collective-permute-start.5
  16.8 2.7 %collective-permute-start.8 = (bf16[80,512]{1,0:T(8,128)(2,1)S(1)}, bf16[80,512]{1,0:T(8,128)(2,1)S(1)}, u32[]{:S(2)}, u32[]{:S(2)}) collective-permute-start(bf16[80,512]{1,0:T(8,128)(2,1)S(1)} %pad_maximum_fusion.3), channel_id=1, source_target_pairs={{0,24},{2,26},{4,28},{6,30},{8,16},{10,18},{12,20},{14,22},{16,8},... | collective-permute-start | bytes 245768 | tf_op jit(solution)/shard_map/ppermute | solution.py:383
  19.5 1.7 %collective-permute-start.6 = (bf16[80,512]{1,0:T(8,128)(2,1)S(1)}, bf16[80,512]{1,0:T(8,128)(2,1)S(1)}, u32[]{:S(2)}, u32[]{:S(2)}) collective-permute-start(bf16[80,512]{1,0:T(8,128)(2,1)S(1)} %pad_maximum_fusion.3), channel_id=1, source_target_pairs={{0,8},{2,10},{4,12},{6,14},{8,0},{10,2},{12,4},{14,6},{16,24},{18,... | collective-permute-start | bytes 245768 | tf_op jit(solution)/shard_map/ppermute | solution.py:383
  21.2 4.7 %fetch.3 = bf16[4,3072,512]{2,1,0:T(8,128)(2,1)S(1)} custom-call(bf16[4,1,3072,512]{3,2,1,0:T(8,128)(2,1)} %bitcast.52), custom_call_target="tpu_custom_call" | custom-call | bytes 25165824 | tf_op jit(solution)/shard_map/fetch/pallas_call | solution.py:47
  25.9 0.5 collective-permute-done.7
  26.6 3.4 %gate_gemm.2 = (f32[2,320,512]{2,1,0:T(8,128)S(1)}, bf16[2,2,1536,512]{3,2,1,0:T(8,128)(2,1)S(1)}) custom-call(s32[3]{0:T(128)S(1)} %pad_add_fusion.where_ref, s32[320,2]{1,0:T(8,128)S(1)} %get-tuple-element.41.ids_ref, bf16[320,1536]{1,0:T(8,128)(2,1)S(1)} %pad_maximum_fusion.rows_ref.own_ref, bf16[4,2,1536,512]{3,2,1,0:T(8,128)(2,1)S(1)} %bitcast.39, ...), custom_call_target="tpu_custom_call" | custom-call | flops 2013265920 | bytes 6291456 | tf_op jit(solution)/shard_map/gate_gemm/pallas_call | solution.py:169
  30.0 3.4 %gate_gemm.3 = (f32[2,160,512]{2,1,0:T(8,128)S(1)}, bf16[1,2,160,512]{3,2,1,0:T(8,128)(2,1)S(1)}) custom-call(s32[3]{0:T(128)S(1)} %pad_add_fusion.where_ref, s32[320,2]{1,0:T(8,128)S(1)} %get-tuple-element.41.ids_ref, bf16[320,1536]{1,0:T(8,128)(2,1)S(1)} %collective-permute-done.9.rows_ref.other_ref, bf16[4,2,1536,512]{3,2,1,0:T(8,128)(2,1)S(1)} %bitcast.40, ...), custom_call_target="tpu_custom_call" | custom-call | flops 2013265920 | bytes 6291456 | tf_op jit(solution)/shard_map/gate_gemm/pallas_call | solution.py:169
  33.4 1.7 %collective-permute-start.10 = (bf16[2,160,512]{2,1,0:T(8,128)(2,1)S(1)}, bf16[2,160,512]{2,1,0:T(8,128)(2,1)S(1)}, u32[]{:S(2)}, u32[]{:S(2)}) collective-permute-start(bf16[2,160,512]{2,1,0:T(8,128)(2,1)S(1)} %bitcast.45), channel_id=1, source_target_pairs={{0,1},{1,0},{2,3},{3,2},{4,5},{5,4},{6,7},{7,6},{8,9},{9,8},{10,11... | collective-permute-start | bytes 983048 | tf_op jit(solution)/shard_map/ppermute | solution.py:395
  35.1 2.8 %up_gemm.3 = (f32[2,160,256]{2,1,0:T(8,128)S(1)}, bf16[1,2,160,256]{3,2,1,0:T(8,128)(2,1)S(1)}) custom-call(s32[3]{0:T(128)S(1)} %pad_add_fusion.where_ref, s32[320,2]{1,0:T(8,128)S(1)} %get-tuple-element.41.ids_ref, bf16[320,1536]{1,0:T(8,128)(2,1)S(1)} %pad_maximum_fusion.rows_ref.own_ref, bf16[320,1536]{1,0:T(8,128)(2,1)S(1)} %collective-permute-done.9.rows_ref.other_ref, ...), custom_call_target="tpu_custom_call" | custom-call | flops 2013265920 | bytes 6291456 | tf_op jit(solution)/shard_map/up_gemm/pallas_call | solution.py:211
  37.9 0.5 collective-permute-start.12
  38.4 2.8 %up_gemm.2 = (f32[2,160,256]{2,1,0:T(8,128)S(1)}, bf16[1,2,160,256]{3,2,1,0:T(8,128)(2,1)S(1)}) custom-call(s32[3]{0:T(128)S(1)} %pad_add_fusion.where_ref, s32[320,2]{1,0:T(8,128)S(1)} %get-tuple-element.41.ids_ref, bf16[320,1536]{1,0:T(8,128)(2,1)S(1)} %pad_maximum_fusion.rows_ref.own_ref, bf16[320,1536]{1,0:T(8,128)(2,1)S(1)} %collective-permute-done.9.rows_ref.other_ref, ...), custom_call_target="tpu_custom_call" | custom-call | flops 2013265920 | bytes 6291456 | tf_op jit(solution)/shard_map/up_gemm/pallas_call | solution.py:211
  41.2 1.7 %collective-permute-start.11 = (bf16[2,160,256]{2,1,0:T(8,128)(2,1)S(1)}, bf16[2,160,256]{2,1,0:T(8,128)(2,1)S(1)}, u32[]{:S(2)}, u32[]{:S(2)}) collective-permute-start(bf16[2,160,256]{2,1,0:T(8,128)(2,1)S(1)} %bitcast.46), channel_id=1, source_target_pairs={{0,1},{1,0},{2,3},{3,2},{4,5},{5,4},{6,7},{7,6},{8,9},{9,8},{10,11... | collective-permute-start | bytes 491528 | tf_op jit(solution)/shard_map/ppermute | solution.py:395
  42.9 2.9 %fetch.4.refs_2_ = bf16[4,256,3072]{2,1,0:T(8,128)(2,1)S(1)} custom-call(bf16[4,2,256,3072]{3,2,1,0:T(8,128)(2,1)} %bitcast.50), custom_call_target="tpu_custom_call" | custom-call | bytes 12582912 | tf_op jit(solution)/shard_map/fetch/pallas_call | solution.py:47
  45.7 1.8 %collective-permute-done.12 = bf16[2,160,256]{2,1,0:T(8,128)(2,1)S(1)} collective-permute-done((bf16[2,160,256]{2,1,0:T(8,128)(2,1)S(1)}, bf16[2,160,256]{2,1,0:T(8,128)(2,1)S(1)}, u32[]{:S(2)}, u32[]{:S(2)}) %collective-permute-start.12) | collective-permute-done | bytes 163872 | tf_op jit(solution)/shard_map/ppermute | solution.py:395
  47.7 2.9 %fetch.5.wd_ref = bf16[4,256,3072]{2,1,0:T(8,128)(2,1)S(1)} custom-call(bf16[4,2,256,3072]{3,2,1,0:T(8,128)(2,1)} %bitcast.51), custom_call_target="tpu_custom_call" | custom-call | bytes 12582912 | tf_op jit(solution)/shard_map/fetch/pallas_call | solution.py:47
  50.8 1.7 %collective-permute-start.13 = (bf16[2,160,256]{2,1,0:T(8,128)(2,1)S(1)}, bf16[2,160,256]{2,1,0:T(8,128)(2,1)S(1)}, u32[]{:S(2)}, u32[]{:S(2)}) collective-permute-start(bf16[2,160,256]{2,1,0:T(8,128)(2,1)S(1)} %multiply_convert_fusion.refs_0_), channel_id=1, source_target_pairs={{0,1},{1,0},{2,3},{3,2},{4,5},{5,4},{6,7},{7,6},{8,9},{9,8},{10,11... | collective-permute-start | bytes 491528 | tf_op jit(solution)/shard_map/ppermute | solution.py:395
  52.8 5.0 %collective-permute-done.13.refs_1_ = bf16[2,160,256]{2,1,0:T(8,128)(2,1)S(1)} collective-permute-done((bf16[2,160,256]{2,1,0:T(8,128)(2,1)S(1)}, bf16[2,160,256]{2,1,0:T(8,128)(2,1)S(1)}, u32[]{:S(2)}, u32[]{:S(2)}) %collective-permute-start.13) | collective-permute-done | bytes 163872 | tf_op jit(solution)/shard_map/ppermute | solution.py:395
  57.9 1.0 pick.1.rows_ref
  58.9 1.2 %collective-permute-done.14.refs_1_ = bf16[2,160,256]{2,1,0:T(8,128)(2,1)S(1)} collective-permute-done((bf16[2,160,256]{2,1,0:T(8,128)(2,1)S(1)}, bf16[2,160,256]{2,1,0:T(8,128)(2,1)S(1)}, u32[]{:S(2)}, u32[]{:S(2)}) %collective-permute-start.14) | collective-permute-done | bytes 163872 | tf_op jit(solution)/shard_map/ppermute | solution.py:395
  60.1 3.6 %first_down.1.refs_0_ = f32[2,320,1536]{2,1,0:T(8,128)S(1)} custom-call(s32[3]{0:T(128)S(1)} %pad_add_fusion.where_ref, s32[320,2]{1,0:T(8,128)S(1)} %get-tuple-element.41.ids_ref, f32[320,2]{1,0:T(8,128)S(1)} %get-tuple-element.42.probs_ref, bf16[2,160,256]{2,1,0:T(8,128)(2,1)S(1)} %multiply_convert_fusion.1.refs_0_, ...), custom_call_target="tpu_custom_call" | custom-call | flops 2013265920 | bytes 6291456 | tf_op jit(solution)/shard_map/first_down/pallas_call | solution.py:288
  63.7 1.5 %down_other.2 = f32[320,768]{1,0:T(8,128)S(1)} custom-call(s32[3]{0:T(128)S(1)} %pad_add_fusion.where_ref, s32[320,2]{1,0:T(8,128)S(1)} %get-tuple-element.41.ids_ref, f32[320,2]{1,0:T(8,128)S(1)} %get-tuple-element.42.probs_ref, bf16[4,320,256]{2,1,0:T(8,128)(2,1)S(1)} %pick.1.rows_ref, bf16[4,256,3072]{2,1,0:T(8,128)(2,1)S(1)} %fetch.5.wd_ref, ...), custom_call_target="tpu_custom_call" | custom-call | flops 503316480 | bytes 1572864 | tf_op jit(solution)/shard_map/down_other/pallas_call | solution.py:330
  65.3 1.5 %down_own.2 = f32[320,768]{1,0:T(8,128)S(1)} custom-call(s32[3]{0:T(128)S(1)} %pad_add_fusion.where_ref, s32[320,2]{1,0:T(8,128)S(1)} %get-tuple-element.41.ids_ref, f32[320,2]{1,0:T(8,128)S(1)} %get-tuple-element.42.probs_ref, bf16[4,320,256]{2,1,0:T(8,128)(2,1)S(1)} %pick.1.rows_ref, bf16[4,256,3072]{2,1,0:T(8,128)(2,1)S(1)} %fetch.5.wd_ref, ...), custom_call_target="tpu_custom_call" | custom-call | flops 503316480 | bytes 1572864 | tf_op jit(solution)/shard_map/down_own/pallas_call | solution.py:330
  66.8 1.1 %collective-permute-done.15 = f32[320,768]{1,0:T(8,128)S(1)} collective-permute-done((f32[320,768]{1,0:T(8,128)S(1)}, f32[320,768]{1,0:T(8,128)S(1)}, u32[]{:S(2)}, u32[]{:S(2)}) %collective-permute-start.15) | collective-permute-done | bytes 983072 | tf_op jit(solution)/shard_map/ppermute | solution.py:383
  67.9 1.5 %down_other.3 = f32[320,768]{1,0:T(8,128)S(1)} custom-call(s32[3]{0:T(128)S(1)} %pad_add_fusion.where_ref, s32[320,2]{1,0:T(8,128)S(1)} %get-tuple-element.41.ids_ref, f32[320,2]{1,0:T(8,128)S(1)} %get-tuple-element.42.probs_ref, bf16[4,320,256]{2,1,0:T(8,128)(2,1)S(1)} %pick.1.rows_ref, bf16[4,256,3072]{2,1,0:T(8,128)(2,1)S(1)} %fetch.5.wd_ref, ...), custom_call_target="tpu_custom_call" | custom-call | flops 503316480 | bytes 1572864 | tf_op jit(solution)/shard_map/down_other/pallas_call | solution.py:330
  69.6 1.6 %collective-permute-start.16 = (bf16[4,40,768]{2,1,0:T(8,128)(2,1)S(1)}, bf16[4,40,768]{2,1,0:T(8,128)(2,1)S(1)}, u32[]{:S(2)}, u32[]{:S(2)}) collective-permute-start(bf16[4,40,768]{2,1,0:T(8,128)(2,1)S(1)} %bitcast.54), channel_id=1, source_target_pairs={{0,4},{2,6},{4,0},{6,2},{8,12},{10,14},{12,8},{14,10},{16,20},{18,... | collective-permute-start | bytes 737288 | tf_op jit(solution)/shard_map/ppermute | solution.py:383
  71.2 1.5 %down_own.3 = f32[320,768]{1,0:T(8,128)S(1)} custom-call(s32[3]{0:T(128)S(1)} %pad_add_fusion.where_ref, s32[320,2]{1,0:T(8,128)S(1)} %get-tuple-element.41.ids_ref, f32[320,2]{1,0:T(8,128)S(1)} %get-tuple-element.42.probs_ref, bf16[4,320,256]{2,1,0:T(8,128)(2,1)S(1)} %pick.1.rows_ref, bf16[4,256,3072]{2,1,0:T(8,128)(2,1)S(1)} %fetch.5.wd_ref, ...), custom_call_target="tpu_custom_call" | custom-call | flops 503316480 | bytes 1572864 | tf_op jit(solution)/shard_map/down_own/pallas_call | solution.py:330
  72.8 5.1 %collective-permute-done.16 = bf16[4,40,768]{2,1,0:T(8,128)(2,1)S(1)} collective-permute-done((bf16[4,40,768]{2,1,0:T(8,128)(2,1)S(1)}, bf16[4,40,768]{2,1,0:T(8,128)(2,1)S(1)}, u32[]{:S(2)}, u32[]{:S(2)}) %collective-permute-start.16) | collective-permute-done | bytes 245792 | tf_op jit(solution)/shard_map/ppermute | solution.py:383
  78.0 2.3 %collective-permute-start.19 = (bf16[40,768]{1,0:T(8,128)(2,1)S(1)}, bf16[40,768]{1,0:T(8,128)(2,1)S(1)}, u32[]{:S(2)}, u32[]{:S(2)}) collective-permute-start(bf16[40,768]{1,0:T(8,128)(2,1)S(1)} %get-tuple-element.84), channel_id=1, source_target_pairs={{0,24},{2,26},{4,28},{6,30},{8,16},{10,18},{12,20},{14,22},{16,8},... | collective-permute-start | bytes 184328 | tf_op jit(solution)/shard_map/ppermute | solution.py:383
  80.3 1.1 %collective-permute-start.18 = (bf16[40,768]{1,0:T(8,128)(2,1)S(1)}, bf16[40,768]{1,0:T(8,128)(2,1)S(1)}, u32[]{:S(2)}, u32[]{:S(2)}) collective-permute-start(bf16[40,768]{1,0:T(8,128)(2,1)S(1)} %get-tuple-element.85), channel_id=1, source_target_pairs={{0,16},{2,18},{4,20},{6,22},{8,24},{10,26},{12,28},{14,30},{16,0},... | collective-permute-start | bytes 184328 | tf_op jit(solution)/shard_map/ppermute | solution.py:383
  81.6 1.6 %collective-permute-start.21 = (bf16[4,40,768]{2,1,0:T(8,128)(2,1)S(1)}, bf16[4,40,768]{2,1,0:T(8,128)(2,1)S(1)}, u32[]{:S(2)}, u32[]{:S(2)}) collective-permute-start(bf16[4,40,768]{2,1,0:T(8,128)(2,1)S(1)} %bitcast.53), channel_id=1, source_target_pairs={{0,4},{2,6},{4,0},{6,2},{8,12},{10,14},{12,8},{14,10},{16,20},{18,... | collective-permute-start | bytes 737288 | tf_op jit(solution)/shard_map/ppermute | solution.py:383
  83.3 1.3 %collective-permute-done.19 = bf16[40,768]{1,0:T(8,128)(2,1)S(1)} collective-permute-done((bf16[40,768]{1,0:T(8,128)(2,1)S(1)}, bf16[40,768]{1,0:T(8,128)(2,1)S(1)}, u32[]{:S(2)}, u32[]{:S(2)}) %collective-permute-start.19) | collective-permute-done | bytes 61472 | tf_op jit(solution)/shard_map/ppermute | solution.py:383
  84.6 2.5 %collective-permute-done.18 = bf16[40,768]{1,0:T(8,128)(2,1)S(1)} collective-permute-done((bf16[40,768]{1,0:T(8,128)(2,1)S(1)}, bf16[40,768]{1,0:T(8,128)(2,1)S(1)}, u32[]{:S(2)}, u32[]{:S(2)}) %collective-permute-start.18) | collective-permute-done | bytes 61472 | tf_op jit(solution)/shard_map/ppermute | solution.py:383
  87.2 1.0 %collective-permute-done.21 = bf16[4,40,768]{2,1,0:T(8,128)(2,1)S(1)} collective-permute-done((bf16[4,40,768]{2,1,0:T(8,128)(2,1)S(1)}, bf16[4,40,768]{2,1,0:T(8,128)(2,1)S(1)}, u32[]{:S(2)}, u32[]{:S(2)}) %collective-permute-start.21) | collective-permute-done | bytes 245792 | tf_op jit(solution)/shard_map/ppermute | solution.py:383
  88.3 1.3 %collective-permute-start.22 = (bf16[40,768]{1,0:T(8,128)(2,1)S(1)}, bf16[40,768]{1,0:T(8,128)(2,1)S(1)}, u32[]{:S(2)}, u32[]{:S(2)}) collective-permute-start(bf16[40,768]{1,0:T(8,128)(2,1)S(1)} %get-tuple-element.86), channel_id=1, source_target_pairs={{0,8},{2,10},{4,12},{6,14},{8,0},{10,2},{12,4},{14,6},{16,24},{18,... | collective-permute-start | bytes 184328 | tf_op jit(solution)/shard_map/ppermute | solution.py:383
  89.6 2.3 %collective-permute-start.24 = (bf16[40,768]{1,0:T(8,128)(2,1)S(1)}, bf16[40,768]{1,0:T(8,128)(2,1)S(1)}, u32[]{:S(2)}, u32[]{:S(2)}) collective-permute-start(bf16[40,768]{1,0:T(8,128)(2,1)S(1)} %get-tuple-element.87), channel_id=1, source_target_pairs={{0,24},{2,26},{4,28},{6,30},{8,16},{10,18},{12,20},{14,22},{16,8},... | collective-permute-start | bytes 184328 | tf_op jit(solution)/shard_map/ppermute | solution.py:383
  91.9 1.2 %collective-permute-done.22 = bf16[40,768]{1,0:T(8,128)(2,1)S(1)} collective-permute-done((bf16[40,768]{1,0:T(8,128)(2,1)S(1)}, bf16[40,768]{1,0:T(8,128)(2,1)S(1)}, u32[]{:S(2)}, u32[]{:S(2)}) %collective-permute-start.22) | collective-permute-done | bytes 61472 | tf_op jit(solution)/shard_map/ppermute | solution.py:383
  93.2 2.5 %collective-permute-done.24 = bf16[40,768]{1,0:T(8,128)(2,1)S(1)} collective-permute-done((bf16[40,768]{1,0:T(8,128)(2,1)S(1)}, bf16[40,768]{1,0:T(8,128)(2,1)S(1)}, u32[]{:S(2)}, u32[]{:S(2)}) %collective-permute-start.24) | collective-permute-done | bytes 61472 | tf_op jit(solution)/shard_map/ppermute | solution.py:383
  95.6 1.4 %collective-permute-done.23 = bf16[40,768]{1,0:T(8,128)(2,1)S(1)} collective-permute-done((bf16[40,768]{1,0:T(8,128)(2,1)S(1)}, bf16[40,768]{1,0:T(8,128)(2,1)S(1)}, u32[]{:S(2)}, u32[]{:S(2)}) %collective-permute-start.23) | collective-permute-done | bytes 61472 | tf_op jit(solution)/shard_map/ppermute | solution.py:383
  97.2 1.3 %collective-permute-done.25 = bf16[20,1536]{1,0:T(8,128)(2,1)S(1)} collective-permute-done((bf16[20,1536]{1,0:T(8,128)(2,1)S(1)}, bf16[20,1536]{1,0:T(8,128)(2,1)S(1)}, u32[]{:S(2)}, u32[]{:S(2)}) %collective-permute-start.25) | collective-permute-done | bytes 61472 | tf_op jit(solution)/shard_map/ppermute | solution.py:383
  98.5 0.7 pad_maximum_fusion.2
  (54 shorter events, 2.2 us)
Async XLA Ops:
  0.0 1.7 %collective-permute-start = (bf16[20,3072]{1,0:T(8,128)(2,1)}, bf16[20,3072]{1,0:T(8,128)(2,1)S(1)}, u32[]{:S(2)}, u32[]{:S(2)}) collective-permute-start(bf16[20,3072]{1,0:T(8,128)(2,1)} %param.6), channel_id=1, source_target_pairs={{0,2},{2,0},{4,6},{6,4},{8,10},{10,8},{12,14},{14,12},{16,18},{18,... | collective-permute-start | bytes 368648 | tf_op jit(solution)/shard_map/ppermute | solution.py:383
  2.7 10.8 %collective-permute-start.4 = (bf16[40,512]{1,0:T(8,128)(2,1)S(1)}, bf16[40,512]{1,0:T(8,128)(2,1)S(1)}, u32[]{:S(2)}, u32[]{:S(2)}) collective-permute-start(bf16[40,512]{1,0:T(8,128)(2,1)S(1)} %pad_maximum_fusion.5), channel_id=1, source_target_pairs={{0,4},{2,6},{4,0},{6,2},{8,12},{10,14},{12,8},{14,10},{16,20},{18,... | collective-permute-start | bytes 122888 | tf_op jit(solution)/shard_map/ppermute | solution.py:383
  5.6 7.9 %collective-permute-start.3 = (bf16[40,1024]{1,0:T(8,128)(2,1)S(1)}, bf16[40,1024]{1,0:T(8,128)(2,1)S(1)}, u32[]{:S(2)}, u32[]{:S(2)}) collective-permute-start(bf16[40,1024]{1,0:T(8,128)(2,1)S(1)} %fusion.4), channel_id=1, source_target_pairs={{0,24},{2,26},{4,28},{6,30},{8,16},{10,18},{12,20},{14,22},{16,8},... | collective-permute-start | bytes 245768 | tf_op jit(solution)/shard_map/ppermute | solution.py:383
  9.3 6.9 %collective-permute-start.2 = (bf16[40,1024]{1,0:T(8,128)(2,1)S(1)}, bf16[40,1024]{1,0:T(8,128)(2,1)S(1)}, u32[]{:S(2)}, u32[]{:S(2)}) collective-permute-start(bf16[40,1024]{1,0:T(8,128)(2,1)S(1)} %fusion.4), channel_id=1, source_target_pairs={{0,16},{2,18},{4,20},{6,22},{8,24},{10,26},{12,28},{14,30},{16,0},... | collective-permute-start | bytes 245768 | tf_op jit(solution)/shard_map/ppermute | solution.py:383
  9.3 6.9 %collective-permute-start.1 = (bf16[40,1024]{1,0:T(8,128)(2,1)S(1)}, bf16[40,1024]{1,0:T(8,128)(2,1)S(1)}, u32[]{:S(2)}, u32[]{:S(2)}) collective-permute-start(bf16[40,1024]{1,0:T(8,128)(2,1)S(1)} %fusion.4), channel_id=1, source_target_pairs={{0,8},{2,10},{4,12},{6,14},{8,0},{10,2},{12,4},{14,6},{16,24},{18,... | collective-permute-start | bytes 245768 | tf_op jit(solution)/shard_map/ppermute | solution.py:383
  16.2 10.2 %collective-permute-start.5 = (bf16[160,1024]{1,0:T(8,128)(2,1)S(1)}, bf16[160,1024]{1,0:T(8,128)(2,1)S(1)}, u32[]{:S(2)}, u32[]{:S(2)}) collective-permute-start(bf16[160,1024]{1,0:T(8,128)(2,1)S(1)} %pad_maximum_fusion.1), channel_id=1, source_target_pairs={{0,4},{2,6},{4,0},{6,2},{8,12},{10,14},{12,8},{14,10},{16,20},{18,... | collective-permute-start | bytes 983048 | tf_op jit(solution)/shard_map/ppermute | solution.py:383
  16.8 9.1 %collective-permute-start.8 = (bf16[80,512]{1,0:T(8,128)(2,1)S(1)}, bf16[80,512]{1,0:T(8,128)(2,1)S(1)}, u32[]{:S(2)}, u32[]{:S(2)}) collective-permute-start(bf16[80,512]{1,0:T(8,128)(2,1)S(1)} %pad_maximum_fusion.3), channel_id=1, source_target_pairs={{0,24},{2,26},{4,28},{6,30},{8,16},{10,18},{12,20},{14,22},{16,8},... | collective-permute-start | bytes 245768 | tf_op jit(solution)/shard_map/ppermute | solution.py:383
  19.5 6.9 %collective-permute-start.7 = (bf16[80,512]{1,0:T(8,128)(2,1)S(1)}, bf16[80,512]{1,0:T(8,128)(2,1)S(1)}, u32[]{:S(2)}, u32[]{:S(2)}) collective-permute-start(bf16[80,512]{1,0:T(8,128)(2,1)S(1)} %pad_maximum_fusion.3), channel_id=1, source_target_pairs={{0,16},{2,18},{4,20},{6,22},{8,24},{10,26},{12,28},{14,30},{16,0},... | collective-permute-start | bytes 245768 | tf_op jit(solution)/shard_map/ppermute | solution.py:383
  19.5 6.9 %collective-permute-start.6 = (bf16[80,512]{1,0:T(8,128)(2,1)S(1)}, bf16[80,512]{1,0:T(8,128)(2,1)S(1)}, u32[]{:S(2)}, u32[]{:S(2)}) collective-permute-start(bf16[80,512]{1,0:T(8,128)(2,1)S(1)} %pad_maximum_fusion.3), channel_id=1, source_target_pairs={{0,8},{2,10},{4,12},{6,14},{8,0},{10,2},{12,4},{14,6},{16,24},{18,... | collective-permute-start | bytes 245768 | tf_op jit(solution)/shard_map/ppermute | solution.py:383
  26.5 3.5 %collective-permute-start.9 = (bf16[320,1536]{1,0:T(8,128)(2,1)S(1)}, bf16[320,1536]{1,0:T(8,128)(2,1)S(1)}, u32[]{:S(2)}, u32[]{:S(2)}) collective-permute-start(bf16[320,1536]{1,0:T(8,128)(2,1)S(1)} %pad_maximum_fusion.rows_ref.own_ref), channel_id=1, source_target_pairs={{0,2},{2,0},{4,6},{6,4},{8,10},{10,8},{12,14},{14,12},{16,18},{18,... | collective-permute-start | bytes 2949128 | tf_op jit(solution)/shard_map/ppermute | solution.py:383
  33.4 14.2 %collective-permute-start.10 = (bf16[2,160,512]{2,1,0:T(8,128)(2,1)S(1)}, bf16[2,160,512]{2,1,0:T(8,128)(2,1)S(1)}, u32[]{:S(2)}, u32[]{:S(2)}) collective-permute-start(bf16[2,160,512]{2,1,0:T(8,128)(2,1)S(1)} %bitcast.45), channel_id=1, source_target_pairs={{0,1},{1,0},{2,3},{3,2},{4,5},{5,4},{6,7},{7,6},{8,9},{9,8},{10,11... | collective-permute-start | bytes 983048 | tf_op jit(solution)/shard_map/ppermute | solution.py:395
  37.9 9.7 %collective-permute-start.12 = (bf16[2,160,256]{2,1,0:T(8,128)(2,1)S(1)}, bf16[2,160,256]{2,1,0:T(8,128)(2,1)S(1)}, u32[]{:S(2)}, u32[]{:S(2)}) collective-permute-start(bf16[2,160,256]{2,1,0:T(8,128)(2,1)S(1)} %bitcast.47), channel_id=1, source_target_pairs={{0,1},{1,0},{2,3},{3,2},{4,5},{5,4},{6,7},{7,6},{8,9},{9,8},{10,11... | collective-permute-start | bytes 491528 | tf_op jit(solution)/shard_map/ppermute | solution.py:395
  41.2 9.4 %collective-permute-start.11 = (bf16[2,160,256]{2,1,0:T(8,128)(2,1)S(1)}, bf16[2,160,256]{2,1,0:T(8,128)(2,1)S(1)}, u32[]{:S(2)}, u32[]{:S(2)}) collective-permute-start(bf16[2,160,256]{2,1,0:T(8,128)(2,1)S(1)} %bitcast.46), channel_id=1, source_target_pairs={{0,1},{1,0},{2,3},{3,2},{4,5},{5,4},{6,7},{7,6},{8,9},{9,8},{10,11... | collective-permute-start | bytes 491528 | tf_op jit(solution)/shard_map/ppermute | solution.py:395
  50.8 7.1 %collective-permute-start.13 = (bf16[2,160,256]{2,1,0:T(8,128)(2,1)S(1)}, bf16[2,160,256]{2,1,0:T(8,128)(2,1)S(1)}, u32[]{:S(2)}, u32[]{:S(2)}) collective-permute-start(bf16[2,160,256]{2,1,0:T(8,128)(2,1)S(1)} %multiply_convert_fusion.refs_0_), channel_id=1, source_target_pairs={{0,1},{1,0},{2,3},{3,2},{4,5},{5,4},{6,7},{7,6},{8,9},{9,8},{10,11... | collective-permute-start | bytes 491528 | tf_op jit(solution)/shard_map/ppermute | solution.py:395
  52.4 7.7 %collective-permute-start.14 = (bf16[2,160,256]{2,1,0:T(8,128)(2,1)S(1)}, bf16[2,160,256]{2,1,0:T(8,128)(2,1)S(1)}, u32[]{:S(2)}, u32[]{:S(2)}) collective-permute-start(bf16[2,160,256]{2,1,0:T(8,128)(2,1)S(1)} %multiply_convert_fusion.1.refs_0_), channel_id=1, source_target_pairs={{0,1},{1,0},{2,3},{3,2},{4,5},{5,4},{6,7},{7,6},{8,9},{9,8},{10,11... | collective-permute-start | bytes 491528 | tf_op jit(solution)/shard_map/ppermute | solution.py:395
  65.2 2.6 %collective-permute-start.15 = (f32[320,768]{1,0:T(8,128)S(1)}, f32[320,768]{1,0:T(8,128)S(1)}, u32[]{:S(2)}, u32[]{:S(2)}) collective-permute-start(f32[320,768]{1,0:T(8,128)S(1)} %down_other.2), channel_id=1, source_target_pairs={{0,2},{2,0},{4,6},{6,4},{8,10},{10,8},{12,14},{14,12},{16,18},{18,... | collective-permute-start | bytes 2949128 | tf_op jit(solution)/shard_map/ppermute | solution.py:383
  69.4 12.1 %collective-permute-start.20 = (f32[320,768]{1,0:T(8,128)S(1)}, f32[320,768]{1,0:T(8,128)S(1)}, u32[]{:S(2)}, u32[]{:S(2)}) collective-permute-start(f32[320,768]{1,0:T(8,128)S(1)} %down_other.3), channel_id=1, source_target_pairs={{0,2},{2,0},{4,6},{6,4},{8,10},{10,8},{12,14},{14,12},{16,18},{18,... | collective-permute-start | bytes 2949128 | tf_op jit(solution)/shard_map/ppermute | solution.py:383
  69.6 8.2 %collective-permute-start.16 = (bf16[4,40,768]{2,1,0:T(8,128)(2,1)S(1)}, bf16[4,40,768]{2,1,0:T(8,128)(2,1)S(1)}, u32[]{:S(2)}, u32[]{:S(2)}) collective-permute-start(bf16[4,40,768]{2,1,0:T(8,128)(2,1)S(1)} %bitcast.54), channel_id=1, source_target_pairs={{0,4},{2,6},{4,0},{6,2},{8,12},{10,14},{12,8},{14,10},{16,20},{18,... | collective-permute-start | bytes 737288 | tf_op jit(solution)/shard_map/ppermute | solution.py:383
  77.9 5.3 %collective-permute-start.17 = (bf16[40,768]{1,0:T(8,128)(2,1)S(1)}, bf16[40,768]{1,0:T(8,128)(2,1)S(1)}, u32[]{:S(2)}, u32[]{:S(2)}) collective-permute-start(bf16[40,768]{1,0:T(8,128)(2,1)S(1)} %get-tuple-element.83), channel_id=1, source_target_pairs={{0,8},{2,10},{4,12},{6,14},{8,0},{10,2},{12,4},{14,6},{16,24},{18,... | collective-permute-start | bytes 184328 | tf_op jit(solution)/shard_map/ppermute | solution.py:383
  78.0 6.6 %collective-permute-start.19 = (bf16[40,768]{1,0:T(8,128)(2,1)S(1)}, bf16[40,768]{1,0:T(8,128)(2,1)S(1)}, u32[]{:S(2)}, u32[]{:S(2)}) collective-permute-start(bf16[40,768]{1,0:T(8,128)(2,1)S(1)} %get-tuple-element.84), channel_id=1, source_target_pairs={{0,24},{2,26},{4,28},{6,30},{8,16},{10,18},{12,20},{14,22},{16,8},... | collective-permute-start | bytes 184328 | tf_op jit(solution)/shard_map/ppermute | solution.py:383
  80.3 6.7 %collective-permute-start.18 = (bf16[40,768]{1,0:T(8,128)(2,1)S(1)}, bf16[40,768]{1,0:T(8,128)(2,1)S(1)}, u32[]{:S(2)}, u32[]{:S(2)}) collective-permute-start(bf16[40,768]{1,0:T(8,128)(2,1)S(1)} %get-tuple-element.85), channel_id=1, source_target_pairs={{0,16},{2,18},{4,20},{6,22},{8,24},{10,26},{12,28},{14,30},{16,0},... | collective-permute-start | bytes 184328 | tf_op jit(solution)/shard_map/ppermute | solution.py:383
  81.6 6.6 %collective-permute-start.21 = (bf16[4,40,768]{2,1,0:T(8,128)(2,1)S(1)}, bf16[4,40,768]{2,1,0:T(8,128)(2,1)S(1)}, u32[]{:S(2)}, u32[]{:S(2)}) collective-permute-start(bf16[4,40,768]{2,1,0:T(8,128)(2,1)S(1)} %bitcast.53), channel_id=1, source_target_pairs={{0,4},{2,6},{4,0},{6,2},{8,12},{10,14},{12,8},{14,10},{16,20},{18,... | collective-permute-start | bytes 737288 | tf_op jit(solution)/shard_map/ppermute | solution.py:383
  88.3 4.9 %collective-permute-start.22 = (bf16[40,768]{1,0:T(8,128)(2,1)S(1)}, bf16[40,768]{1,0:T(8,128)(2,1)S(1)}, u32[]{:S(2)}, u32[]{:S(2)}) collective-permute-start(bf16[40,768]{1,0:T(8,128)(2,1)S(1)} %get-tuple-element.86), channel_id=1, source_target_pairs={{0,8},{2,10},{4,12},{6,14},{8,0},{10,2},{12,4},{14,6},{16,24},{18,... | collective-permute-start | bytes 184328 | tf_op jit(solution)/shard_map/ppermute | solution.py:383
  89.6 6.0 %collective-permute-start.24 = (bf16[40,768]{1,0:T(8,128)(2,1)S(1)}, bf16[40,768]{1,0:T(8,128)(2,1)S(1)}, u32[]{:S(2)}, u32[]{:S(2)}) collective-permute-start(bf16[40,768]{1,0:T(8,128)(2,1)S(1)} %get-tuple-element.87), channel_id=1, source_target_pairs={{0,24},{2,26},{4,28},{6,30},{8,16},{10,18},{12,20},{14,22},{16,8},... | collective-permute-start | bytes 184328 | tf_op jit(solution)/shard_map/ppermute | solution.py:383
  91.9 5.1 %collective-permute-start.23 = (bf16[40,768]{1,0:T(8,128)(2,1)S(1)}, bf16[40,768]{1,0:T(8,128)(2,1)S(1)}, u32[]{:S(2)}, u32[]{:S(2)}) collective-permute-start(bf16[40,768]{1,0:T(8,128)(2,1)S(1)} %get-tuple-element.88), channel_id=1, source_target_pairs={{0,16},{2,18},{4,20},{6,22},{8,24},{10,26},{12,28},{14,30},{16,0},... | collective-permute-start | bytes 184328 | tf_op jit(solution)/shard_map/ppermute | solution.py:383
  97.1 1.3 %collective-permute-start.25 = (bf16[20,1536]{1,0:T(8,128)(2,1)S(1)}, bf16[20,1536]{1,0:T(8,128)(2,1)S(1)}, u32[]{:S(2)}, u32[]{:S(2)}) collective-permute-start(bf16[20,1536]{1,0:T(8,128)(2,1)S(1)} %broadcast_select_fusion.2), channel_id=1, source_target_pairs={{0,2},{2,0},{4,6},{6,4},{8,10},{10,8},{12,14},{14,12},{16,18},{18,... | collective-permute-start | bytes 184328 | tf_op jit(solution)/shard_map/ppermute | solution.py:383
